TPU v7x, 128 devices: a whole 4x4x4 slice. The times are simulated.
128 devices in a mesh: phi: 16 (over y_hi, z, core), gz: 8 (over y_lo, x).
Axes of the slice: x: 4, y: 4 (y_hi: 2, y_lo: 2; y = y_hi * 2 + y_lo), z: 4, core: 2. Of those that a mesh axis runs over, the one named last changes fastest.
Arguments:
- electric_radial: float32 [192, 128, 2048], P('gz', None, 'phi'), may hold values from -6 to 6
- electric_azimuth: float32 [192, 128, 2048], P('gz', None, 'phi'), may hold values from -6 to 6
- electric_height: float32 [192, 128, 2048], P('gz', None, 'phi'), may hold values from -6 to 6
- magnetic_radial: float32 [192, 128, 2048], P('gz', None, 'phi'), may hold values from -6 to 6
- magnetic_azimuth: float32 [192, 128, 2048], P('gz', None, 'phi'), may hold values from -6 to 6
- magnetic_height: float32 [192, 128, 2048], P('gz', None, 'phi'), may hold values from -6 to 6
- material: int32 [192, 128, 2048], P('gz', None, 'phi'), may hold values from 0 to 7
- permittivity: float32 [8], replicated, may hold values from 1 to 10
- conductivity: float32 [8], replicated, may hold values from 0.05 to 5
- mode_cutoff: int32 [32], replicated, may hold values from 1 to 127, as said below
Outputs:
- updated_electric_radial: float32 [192, 128, 2048], P('gz', None, 'phi')
- updated_electric_azimuth: float32 [192, 128, 2048], P('gz', None, 'phi')
- updated_electric_height: float32 [192, 128, 2048], P('gz', None, 'phi')
- updated_magnetic_radial: float32 [192, 128, 2048], P('gz', None, 'phi')
- updated_magnetic_azimuth: float32 [192, 128, 2048], P('gz', None, 'phi')
- updated_magnetic_height: float32 [192, 128, 2048], P('gz', None, 'phi')
Inputs may be any that keep to these rules, and one draw needn't show every extreme that they name: `mode_cutoff`: cutoffs never fall from one filtered row to the next outward, and the outermost filtered row's cutoff is 127.
All inputs are finite; a program needn't handle non-finite values.
Results may differ from a plain program's by a relative error of at most 0.00005.
Values sent between devices are 32-bit elements; how exact they have to be, the bound alone decides.
A program may use at most 128 MiB of HBM per device.

v0:
```python
import math

import jax
import jax.numpy as jnp
from jax import lax
from jax.sharding import PartitionSpec as P

KMAX = 128
NF = 32
NMAT = 8


inner_radius = 64.0
time_step = 0.2


def shifted(block, axis, distance):
    devices = range(lax.axis_size(axis))
    route = [((i - distance) % len(devices), i) for i in devices]
    return lax.ppermute(block, axis, route)


def shifted_2(block, axis, distance):
    devices = range(lax.axis_size(axis))
    route = [(i - distance, i) for i in devices if i - distance in devices]
    return lax.ppermute(block, axis, route)


def radial_forward(values):
    zero_slab = jnp.zeros_like(values[:, :1, :])
    return jnp.concatenate([values[:, 1:, :], zero_slab], axis=1) - values


def radial_backward(values):
    zero_slab = jnp.zeros_like(values[:, :1, :])
    return values - jnp.concatenate([zero_slab, values[:, :-1, :]], axis=1)


def ahead_azimuth(values, border):
    return jnp.concatenate([values[:, :, 1:], border[:, :, None]], axis=2) - values


def behind_azimuth(values, border):
    return values - jnp.concatenate([border[:, :, None], values[:, :, :-1]], axis=2)


def ahead_height(values, border):
    return jnp.concatenate([values[1:], border[None]], axis=0) - values


def behind_height(values, border):
    return values - jnp.concatenate([border[None], values[:-1]], axis=0)


def cycle_basis(offset, length, cycle_size):
    columns = offset + jnp.arange(length, dtype=jnp.int32)
    mode_index = jnp.arange(KMAX, dtype=jnp.int32)
    angles = (columns[:, None] * mode_index[None, :] % cycle_size).astype(jnp.float32) * (
        2.0 * math.pi / cycle_size
    )
    return jnp.concatenate([jnp.cos(angles), jnp.sin(angles)], axis=1)


def mode_weights(cutoffs, cycle_size):
    mode_index = jnp.arange(KMAX, dtype=jnp.int32)
    scaled = jnp.where(mode_index == 0, 1.0, 2.0).astype(jnp.float32) / cycle_size
    weights = jnp.where(mode_index[None, :] <= cutoffs[:, None], scaled[None, :], 0.0)
    return jnp.concatenate([weights, weights], axis=1)


def transform(block, basis):
    flat = block.reshape(-1, block.shape[-1])
    result = jnp.dot(
        flat, basis, precision=lax.Precision.HIGHEST, preferred_element_type=jnp.float32
    )
    return result.reshape(block.shape[:-1] + (basis.shape[1],))


def synthesize(spectrum, basis):
    flat = spectrum.reshape(-1, spectrum.shape[-1])
    result = jnp.dot(
        flat, basis.T, precision=lax.Precision.HIGHEST, preferred_element_type=jnp.float32
    )
    return result.reshape(spectrum.shape[:-1] + (basis.shape[0],))


def cycle_filter(stacked, mode_cutoff):
    cycle_count = lax.axis_size("phi")
    local_width = stacked.shape[3]
    cycle_size = cycle_count * local_width
    offset = lax.axis_index("phi") * local_width
    weights = mode_weights(mode_cutoff, cycle_size)
    local_basis = cycle_basis(offset, local_width, cycle_size)
    portion = lax.all_gather(stacked, "phi", axis=3, tiled=True)
    spectrum = transform(portion, cycle_basis(jnp.int32(0), portion.shape[3], cycle_size))
    return synthesize(spectrum * weights[None, None], local_basis)


def filter_three(first, second, third, mode_cutoff):
    stacked = jnp.stack([first[:, :NF], second[:, :NF], third[:, :NF]])
    filtered = cycle_filter(stacked, mode_cutoff)
    return (
        jnp.concatenate([filtered[0], first[:, NF:]], axis=1),
        jnp.concatenate([filtered[1], second[:, NF:]], axis=1),
        jnp.concatenate([filtered[2], third[:, NF:]], axis=1),
    )


def local(
    electric_radial,
    electric_azimuth,
    electric_height,
    magnetic_radial,
    magnetic_azimuth,
    magnetic_height,
    material,
    permittivity,
    conductivity,
    mode_cutoff,
):
    local_width = electric_radial.shape[2]
    radial_rows = electric_radial.shape[1]
    node_radius = (inner_radius + jnp.arange(radial_rows, dtype=jnp.float32))[None, :, None]
    center_radius = node_radius + 0.5
    angle_step = 2.0 * math.pi / (lax.axis_size("phi") * local_width)
    border_height, border_radial = shifted(
        (electric_height[:, :, 0], electric_radial[:, :, 0]), "phi", -1
    )
    upper_azimuth, upper_radial = shifted_2((electric_azimuth[0], electric_radial[0]), "gz", -1)
    radial_half = magnetic_radial - time_step * (
        ahead_azimuth(electric_height, border_height) / (node_radius * angle_step)
        - ahead_height(electric_azimuth, upper_azimuth)
    )
    azimuth_half = magnetic_azimuth - time_step * (
        ahead_height(electric_radial, upper_radial) - radial_forward(electric_height)
    )
    height_half = magnetic_height - time_step * (
        radial_forward(node_radius * electric_azimuth) / center_radius
        - ahead_azimuth(electric_radial, border_radial) / (center_radius * angle_step)
    )
    new_hr, new_hp, new_hz = filter_three(radial_half, azimuth_half, height_half, mode_cutoff)
    epsilon = jnp.zeros(material.shape, jnp.float32)
    sigma_cell = jnp.zeros(material.shape, jnp.float32)
    for number in range(NMAT):
        epsilon = jnp.where(material == number, permittivity[number], epsilon)
        sigma_cell = jnp.where(material == number, conductivity[number], sigma_cell)
    losses = sigma_cell * time_step / (2.0 * epsilon)
    keep_factor = (1.0 - losses) / (1.0 + losses)
    drive_factor = time_step / (epsilon * (1.0 + losses))
    before_height, before_radial = shifted((new_hz[:, :, -1], new_hr[:, :, -1]), "phi", 1)
    lower_azimuth, lower_radial = shifted_2((new_hp[-1], new_hr[-1]), "gz", 1)
    radial_next = keep_factor * electric_radial + drive_factor * (
        behind_azimuth(new_hz, before_height) / (center_radius * angle_step)
        - behind_height(new_hp, lower_azimuth)
    )
    azimuth_next = keep_factor * electric_azimuth + drive_factor * (
        behind_height(new_hr, lower_radial) - radial_backward(new_hp)
    )
    height_next = keep_factor * electric_height + drive_factor * (
        radial_backward(center_radius * new_hp) / node_radius
        - behind_azimuth(new_hr, before_radial) / (node_radius * angle_step)
    )
    new_er, new_ep, new_ez = filter_three(radial_next, azimuth_next, height_next, mode_cutoff)
    return (new_er, new_ep, new_ez, new_hr, new_hp, new_hz)


def solution(mesh):
    placed = (
        P("gz", None, "phi"),
        P("gz", None, "phi"),
        P("gz", None, "phi"),
        P("gz", None, "phi"),
        P("gz", None, "phi"),
        P("gz", None, "phi"),
        P("gz", None, "phi"),
        P(),
        P(),
        P(),
    )
    return jax.shard_map(
        local,
        mesh=mesh,
        in_specs=placed,
        out_specs=(
            P("gz", None, "phi"),
            P("gz", None, "phi"),
            P("gz", None, "phi"),
            P("gz", None, "phi"),
            P("gz", None, "phi"),
            P("gz", None, "phi"),
        ),
        check_vma=False,
    )
```

profile of v0, /device:TPU:1, one launch (start us, length us, event | category | flops | bytes accessed | tf_op | source)
XLA Modules:
  0.0 429.9 jit_solution(6858078280458074750)
XLA Ops:
  7.2 2.0 copy.33
  11.2 6.2 %collective-permute-start.3 = (f32[24,128]{1,0:T(8,128)S(1)}, f32[24,128]{1,0:T(8,128)S(1)}, u32[]{:S(2)}, u32[]{:S(2)}) collective-permute-start(f32[24,128]{1,0:T(8,128)S(1)} %bitcast.96), channel_id=1, source_target_pairs={{8,0},{16,8},{24,16},{32,24},{40,32},{48,40},{56,48},{64,56},{72,6... | collective-permute-start | bytes 36872 | tf_op jit(solution)/shard_map/ppermute | solution.py:20
  23.3 1.6 slice.184
  26.2 1.6 slice.194
  27.8 1.7 copy.29
  29.5 1.7 copy.27
  31.2 5.6 %fusion.14 = (f32[24,128,128]{2,1,0:T(8,128)S(1)}, f32[24,128,128]{2,1,0:T(8,128)S(1)}, f32[24,128,128]{2,1,0:T(8,128)S(1)}) fusion(f32[24,128,128]{2,1,0:T(8,128)} %param.13, f32[24,128,128]{2,1,0:T(8,128)S(1)} %copy-done.1, f32[24,128,1]{2,1,0:T(8,128)} %copy.27, f32[24,128,127]{2,1,0:T(8,128)} %slice.184, f32[24,128,128]{2,1,0:T(8,128)} %param.11, ...), kind=kLoop, calls=%fused_computation.37 | loop fusion | flops 5898240 | bytes 18863104 | tf_op jit(solution)/shard_map/sub | solution.py:130
  37.0 2.3 copy-done.20
  45.1 5.0 %fusion.41 = (f32[2048,128]{1,0:T(8,128)}, f32[2048,128]{1,0:T(8,128)}) fusion(), kind=kLoop, calls=%fused_computation.93 | loop fusion | flops 3670016 | bytes 2097152 | tf_op jit(solution)/shard_map/sin | solution.py:61
  50.1 1.5 slice.240
  55.0 118.5 %all-gather.3.cloned.1.call-done = f32[3,24,32,2048]{3,2,1,0:T(8,128)} async-done(((f32[3,24,32,128]{3,2,1,0:T(8,128)}), f32[3,24,32,2048]{3,2,1,0:T(8,128)}) %all-gather.3.cloned.1.call-update) | async-done | bytes 18874384 | tf_op jit(solution)/shard_map/all_gather | solution.py:94
  173.5 18.5 %fusion.2 = f32[3,24,32,256]{3,2,1,0:T(8,128)S(1)} fusion(f32[3,24,32,2048]{3,2,1,0:T(8,128)} %all-gather.3.cloned.1.call-done, f32[2048,128]{1,0:T(8,128)} %get-tuple-element.50, f32[2048,128]{1,0:T(8,128)} %get-tuple-element.51, f32[32,256]{1,0:T(8,128)S(1)} %pad_maximum_fusion.11), kind=kOutput, calls=%fused_computation.24 | convolution fusion | flops 14496628736 | bytes 23363584 | tf_op jit(solution)/shard_map/dot_general | solution.py:73
  192.0 2.0 fusion.44
  204.0 3.7 collective-permute-start.6
  208.3 3.1 collective-permute-start.5
  212.0 2.4 copy.31
  214.4 2.4 copy.30
  216.8 15.9 %fusion.28 = (f32[24,128,128]{2,1,0:T(8,128)S(1)}, f32[24,128,128]{2,1,0:T(8,128)S(1)}, pred[24,128,128]{2,1,0:T(8,128)(4,1)S(1)}, pred[24,128,128]{2,1,0:T(8,12...) fusion(f32[23,128,128]{2,1,0:T(8,128)} %fusion.34, ...), kind=kLoop, calls=%fused_computation.57 | loop fusion | flops 16121856 | bytes 17289280 | tf_op jit(solution)/shard_map/add | solution.py:156
  236.3 14.9 %fusion.25 = (f32[24,128,128]{2,1,0:T(8,128)S(1)}, f32[24,128,128]{2,1,0:T(8,128)}) fusion(f32[24,128,127]{2,1,0:T(8,128)S(1)} %copy-done.13, f32[24,128,1]{2,1,0:T(8,128)S(1)} %copy-done.14, f32[24,128,128]{2,1,0:T(8,128)S(1)} %get-tuple-element.16, f32[23,128,128]{2,1,0:T(8,128)S(1)} %copy-done.26, f32[1,128,128]{2,1,0:T(8,128)} %bitcast.34, ...), kind=kLoop, calls=%fused_computation.52 | loop fusion | flops 13369344 | bytes 14156352 | tf_op jit(solution)/shard_map/add | solution.py:152
  251.3 13.2 %fusion.32 = f32[24,128,128]{2,1,0:T(8,128)S(1)} fusion(f32[24,128,128]{2,1,0:T(8,128)S(1)} %get-tuple-element.7, f32[24,128,127]{2,1,0:T(8,128)S(1)} %copy-done.15, f32[24,128,1]{2,1,0:T(8,128)S(1)} %copy-done.18, f32[24,127,128]{2,1,0:T(8,128)S(1)} %bitcast.87, f32[24,128,128]{2,1,0:T(8,128)S(1)} %copy-done.2, f32[128]{0:T(128)S(1)} %copy-done.42, ...), kind=kLoop, calls=%fused_computation.62 | loop fusion | flops 13369344 | bytes 12572224 | tf_op jit(solution)/shard_map/add | solution.py:159
  266.0 2.4 slice.257
  269.6 127.1 %all-gather.5.cloned.1.call-done = f32[3,24,32,2048]{3,2,1,0:T(8,128)} async-done(((f32[3,24,32,128]{3,2,1,0:T(8,128)}), f32[3,24,32,2048]{3,2,1,0:T(8,128)}) %all-gather.5.cloned.1.call-update) | async-done | bytes 18874384 | tf_op jit(solution)/shard_map/all_gather | solution.py:94
  396.7 18.2 %fusion.3 = f32[3,24,32,256]{3,2,1,0:T(8,128)S(1)} fusion(f32[3,24,32,2048]{3,2,1,0:T(8,128)} %all-gather.5.cloned.1.call-done, f32[2048,128]{1,0:T(8,128)S(1)} %copy-done.8, f32[2048,128]{1,0:T(8,128)S(1)} %copy-done.9, f32[32,256]{1,0:T(8,128)S(1)} %copy-done.30), kind=kOutput, calls=%fused_computation.25 | convolution fusion | flops 14496628736 | bytes 23363584 | tf_op jit(solution)/shard_map/dot_general | solution.py:73
  414.9 2.0 fusion.43
  (153 shorter events, 41.8 us)
Async XLA Ops:
  7.2 166.3 %all-gather.3.cloned.1.call-start = ((), (), s32[]{:S(2)}) async-start(), calls=%async_computation | async-start | bytes 20054016 | tf_op jit(solution)/shard_map/all_gather | solution.py:94
  9.3 20.2 %collective-permute-start = (f32[24,128]{1,0:T(8,128)S(1)}, f32[24,128]{1,0:T(8,128)S(1)}, u32[]{:S(2)}, u32[]{:S(2)}) collective-permute-start(f32[24,128]{1,0:T(8,128)S(1)} %bitcast.94), channel_id=1, source_target_pairs={{8,0},{16,8},{24,16},{32,24},{40,32},{48,40},{56,48},{64,56},{72,6... | collective-permute-start | bytes 36872 | tf_op jit(solution)/shard_map/ppermute | solution.py:20
  11.2 16.6 %collective-permute-start.3 = (f32[24,128]{1,0:T(8,128)S(1)}, f32[24,128]{1,0:T(8,128)S(1)}, u32[]{:S(2)}, u32[]{:S(2)}) collective-permute-start(f32[24,128]{1,0:T(8,128)S(1)} %bitcast.96), channel_id=1, source_target_pairs={{8,0},{16,8},{24,16},{32,24},{40,32},{48,40},{56,48},{64,56},{72,6... | collective-permute-start | bytes 36872 | tf_op jit(solution)/shard_map/ppermute | solution.py:20
  17.4 13.7 %collective-permute-start.2 = (f32[128,128]{1,0:T(8,128)S(1)}, f32[128,128]{1,0:T(8,128)S(1)}, u32[]{:S(2)}, u32[]{:S(2)}) collective-permute-start(f32[128,128]{1,0:T(8,128)S(1)} %slice_bitcast_fusion.6), channel_id=1, source_target_pairs={{1,0},{2,1},{3,2},{4,3},{5,4},{6,5},{7,6},{9,8},{10,9},{11,10},{12... | collective-permute-start | bytes 196616 | tf_op jit(solution)/shard_map/ppermute | solution.py:26
  18.7 12.4 %collective-permute-start.1 = (f32[128,128]{1,0:T(8,128)S(1)}, f32[128,128]{1,0:T(8,128)S(1)}, u32[]{:S(2)}, u32[]{:S(2)}) collective-permute-start(f32[128,128]{1,0:T(8,128)S(1)} %slice_bitcast_fusion.7), channel_id=1, source_target_pairs={{1,0},{2,1},{3,2},{4,3},{5,4},{6,5},{7,6},{9,8},{10,9},{11,10},{12... | collective-permute-start | bytes 196616 | tf_op jit(solution)/shard_map/ppermute | solution.py:26
  20.1 16.9 %copy-start.43 = (f32[128]{0:T(128)}, f32[128]{0:T(128)S(1)}, u32[]{:S(2)}) copy-start(f32[128]{0:T(128)S(1)} %get-tuple-element.49) | copy-start | bytes 1540
  43.1 353.6 %all-gather.5.cloned.1.call-start = ((), (), s32[]{:S(2)}) async-start(), calls=%async_computation.1 | async-start | bytes 20054016 | tf_op jit(solution)/shard_map/all_gather | solution.py:94
  44.8 128.7 %copy-start.29 = (f32[32,256]{1,0:T(8,128)}, f32[32,256]{1,0:T(8,128)S(1)}, u32[]{:S(2)}) copy-start(f32[32,256]{1,0:T(8,128)S(1)} %pad_maximum_fusion.11) | copy-start | bytes 98308
  45.1 146.9 %copy-start.32 = (f32[128,128]{1,0:T(8,128)}, f32[128,128]{1,0:T(8,128)S(1)}, u32[]{:S(2)}) copy-start(f32[128,128]{1,0:T(8,128)S(1)} %get-tuple-element.44) | copy-start | bytes 196612
  45.1 146.9 %copy-start.34 = (f32[128,128]{1,0:T(8,128)}, f32[128,128]{1,0:T(8,128)S(1)}, u32[]{:S(2)}) copy-start(f32[128,128]{1,0:T(8,128)S(1)} %get-tuple-element.45) | copy-start | bytes 196612
  204.0 10.4 %collective-permute-start.4 = (f32[24,128]{1,0:T(8,128)S(1)}, f32[24,128]{1,0:T(8,128)}, u32[]{:S(2)}, u32[]{:S(2)}) collective-permute-start(f32[24,128]{1,0:T(8,128)S(1)} %fusion.5), channel_id=1, source_target_pairs={{120,0},{0,8},{8,16},{16,24},{24,32},{32,40},{40,48},{48,56},{56,6... | collective-permute-start | bytes 36872 | tf_op jit(solution)/shard_map/ppermute | solution.py:20
  204.0 7.4 %collective-permute-start.7 = (f32[24,128]{1,0:T(8,128)S(1)}, f32[24,128]{1,0:T(8,128)S(1)}, u32[]{:S(2)}, u32[]{:S(2)}) collective-permute-start(f32[24,128]{1,0:T(8,128)S(1)} %fusion.9), channel_id=1, source_target_pairs={{120,0},{0,8},{8,16},{16,24},{24,32},{32,40},{40,48},{48,56},{56,6... | collective-permute-start | bytes 36872 | tf_op jit(solution)/shard_map/ppermute | solution.py:20
  204.0 12.8 %collective-permute-start.6 = (f32[128,128]{1,0:T(8,128)}, f32[128,128]{1,0:T(8,128)}, u32[]{:S(2)}, u32[]{:S(2)}) collective-permute-start(f32[128,128]{1,0:T(8,128)} %fusion.53), channel_id=1, source_target_pairs={{0,1},{1,2},{2,3},{3,4},{4,5},{5,6},{6,7},{8,9},{9,10},{10,11},{11... | collective-permute-start | bytes 196616 | tf_op jit(solution)/shard_map/ppermute | solution.py:26
  208.3 25.6 %collective-permute-start.5 = (f32[128,128]{1,0:T(8,128)}, f32[128,128]{1,0:T(8,128)}, u32[]{:S(2)}, u32[]{:S(2)}) collective-permute-start(f32[128,128]{1,0:T(8,128)} %fusion.54), channel_id=1, source_target_pairs={{0,1},{1,2},{2,3},{3,4},{4,5},{5,6},{6,7},{8,9},{9,10},{10,11},{11... | collective-permute-start | bytes 196616 | tf_op jit(solution)/shard_map/ppermute | solution.py:26
  216.8 17.1 %copy-start.14 = (f32[24,128,1]{2,1,0:T(8,128)S(1)}, f32[24,128,1]{2,1,0:T(8,128)}, u32[]{:S(2)}) copy-start(f32[24,128,1]{2,1,0:T(8,128)} %copy.30) | copy-start | bytes 36868
  216.8 17.1 %copy-start.26 = (f32[23,128,128]{2,1,0:T(8,128)S(1)}, f32[23,128,128]{2,1,0:T(8,128)}, u32[]{:S(2)}) copy-start(f32[23,128,128]{2,1,0:T(8,128)} %fusion.33) | copy-start | bytes 4521988
  232.7 18.6 %copy-start.4 = (f32[24,128,128]{2,1,0:T(8,128)}, f32[24,128,128]{2,1,0:T(8,128)S(1)}, u32[]{:S(2)}) copy-start(f32[24,128,128]{2,1,0:T(8,128)S(1)} %get-tuple-element.16) | copy-start | bytes 4718596
  232.7 18.5 %copy-start.25 = (f32[24,128,128]{2,1,0:T(8,128)}, f32[24,128,128]{2,1,0:T(8,128)S(1)}, u32[]{:S(2)}) copy-start(f32[24,128,128]{2,1,0:T(8,128)S(1)} %get-tuple-element.7) | copy-start | bytes 4718596
  236.3 15.1 %copy-start.40 = (f32[128]{0:T(128)S(1)}, f32[128]{0:T(128)}, u32[]{:S(2)}) copy-start(f32[128]{0:T(128)} %copy-done.39) | copy-start | bytes 1540
  269.6 127.1 %copy-start.8 = (f32[2048,128]{1,0:T(8,128)S(1)}, f32[2048,128]{1,0:T(8,128)}, u32[]{:S(2)}) copy-start(f32[2048,128]{1,0:T(8,128)} %get-tuple-element.50) | copy-start | bytes 3145732
  269.6 127.1 %copy-start.9 = (f32[2048,128]{1,0:T(8,128)S(1)}, f32[2048,128]{1,0:T(8,128)}, u32[]{:S(2)}) copy-start(f32[2048,128]{1,0:T(8,128)} %get-tuple-element.51) | copy-start | bytes 3145732
  269.6 127.1 %copy-start.30 = (f32[32,256]{1,0:T(8,128)S(1)}, f32[32,256]{1,0:T(8,128)}, u32[]{:S(2)}) copy-start(f32[32,256]{1,0:T(8,128)} %copy-done.29) | copy-start | bytes 98308
  269.6 145.3 %copy-start.33 = (f32[128,128]{1,0:T(8,128)S(1)}, f32[128,128]{1,0:T(8,128)}, u32[]{:S(2)}) copy-start(f32[128,128]{1,0:T(8,128)} %copy-done.32) | copy-start | bytes 196612
  269.6 145.4 %copy-start.35 = (f32[128,128]{1,0:T(8,128)S(1)}, f32[128,128]{1,0:T(8,128)}, u32[]{:S(2)}) copy-start(f32[128,128]{1,0:T(8,128)} %copy-done.34) | copy-start | bytes 196612
  (33 other events, 162.8 us)
Sparse Core Ops, SparseCore 0:
  43.2 130.2 all-gather.2
  266.2 130.4 all-gather.4
where the time goes:
time: 431 us; the launch traced here: 430 us
  waiting for transfers between devices  246 us (57%)
  other arithmetic  71.7 us (17%)
  matrix products  40.8 us (9%)
  local copies, waits for them, and re-layouts  39.9 us (9%)
  starting transfers between devices  17.3 us (4%)
  between operations  14.7 us (3%)
    all_gather x2, waiting for transfers between devices, cycle_filter(): portion = lax.all_gather(stacked, 'phi', axis=3, tiled=True)  246 us
    dot_general x2, matrix products, transform(): jnp.dot(flat, basis, precision=lax.Precision.HIGHEST, preferred_element_t...  36.8 us
    add x1, other arithmetic, local(): keep_factor * electric_azimuth  15.9 us
    add x1, other arithmetic, local(): keep_factor * electric_radial  14.9 us
    unnamed x94, local copies, waits for them, and re-layouts  14.4 us
    add x1, other arithmetic, local(): keep_factor * electric_height  13.2 us
    ppermute x4, starting transfers between devices, shifted_2(): return lax.ppermute(block, axis, route)  9.37 us
  transfers between devices with their start and end apart: 10, of which 2 were waited for; matrix products, arithmetic and copies ran while one was open for 11% of the time, Pallas kernels for 0%

commit v1 on v0

v1 whole, which is shorter than its diff:
```python
import functools
import math

import jax
import jax.numpy as jnp
import numpy as np
from jax import lax
from jax.experimental import pallas as pl
from jax.experimental.pallas import tpu as pltpu
from jax.sharding import PartitionSpec as P

KMAX = 128
NF = 32
NMAT = 8
NPHI = 2048
NR = 128
LAYERS = 24
WIDTH = 128
CHUNKS = 3
PER_CHUNK = 8
HALF = 4
HALO_R = 32

inner_radius = 64.0
dt = 0.2
dphi = 2.0 * math.pi / NPHI
MESH = pl.DeviceIdType.MESH
F32 = jnp.float32
BF16 = jnp.bfloat16

C_DT_RN, C_UP, C_HERE, C_DT_RC, C_RC, C_KEEP_PREV, C_P, C_Q, C_RN = range(9)
ST_A, ST_1A, ST_1B, ST_2A, ST_2B, ST_C, ST_3A, ST_3B, ST_4A, ST_4B, ST_Z = range(11)
NSTAGE = 13
B_P1I, B_P1O, B_ER, B_EA, B_P2, B_HI, B_HO = range(7)


def basis_tables():
    j = np.arange(WIDTH, dtype=np.float64)[:, None]
    m = np.arange(KMAX, dtype=np.float64)[None, :]
    a = 2.0 * np.pi * j * m / NPHI
    b = 2.0 * np.pi * (j - 1.0) * m / NPHI
    base = np.stack([np.cos(a), np.sin(a), np.cos(a) - np.cos(b), np.sin(a) - np.sin(b)])
    turn = 2.0 * np.pi * ((np.arange(16)[:, None] * WIDTH * np.arange(KMAX)[None, :]) % NPHI) / NPHI
    phase = np.stack([np.cos(turn), np.sin(turn)])
    return base.astype(np.float32), phase.astype(np.float32)


def split(x):
    hi = x.astype(BF16)
    lo = (x - hi.astype(F32)).astype(BF16)
    return hi, lo


def dot3(x, b_hi, b_lo):
    hi, lo = split(x)
    out = jnp.dot(hi, b_hi, preferred_element_type=F32)
    out += jnp.dot(lo, b_hi, preferred_element_type=F32)
    out += jnp.dot(hi, b_lo, preferred_element_type=F32)
    return out


def kernel(
    er_h, ea_h, eh_h, mr_h, mp_h, mz_h, mat_h, perm, cond, cut, base, phase,
    o_er, o_ea, o_eh, o_hr, o_hp, o_hz,
    er, ea, eh, mr, mp, mz, mat,
    coef, ktab, wts, fwd, inv,
    p1s, p1r, p2s, p2r,
    g, ra, s, r1, r2, u, rc_buf, t, v, v2, hf, ho, ki,
    in_sem, send, recv, bsend, brecv,
):
    phi = lax.axis_index("phi")
    gz = lax.axis_index("gz")
    q = phi % 2
    z = (phi // 2) % 4
    hi_bit = z // 2
    low_bit = z % 2
    gray = (hi_bit + low_bit) % 2
    sib = phi + 1 - 2 * q
    chip_z1 = z + 1 - 2 * low_bit
    chip_z3 = 3 - z
    top_y = phi // 8
    dev_z1 = top_y * 8 + chip_z1 * 2 + q
    dev_z3 = top_y * 8 + chip_z3 * 2 + q
    dev_y = (phi + 8) % 16
    nxt = (phi + 1) % 16
    prv = (phi + 15) % 16
    up = (gz + 1) % 8
    down = (gz + 7) % 8
    f1, f2 = gray, hi_bit
    g1, g2 = hi_bit, gray

    lane = lax.broadcasted_iota(jnp.int32, (1, 128), 1)

    loads = []
    RI = 40
    for n, (src, dst, k) in enumerate(
        [(eh_h, eh, LAYERS), (er_h, er, LAYERS), (ea_h, ea, LAYERS), (mr_h, mr, 0), (mp_h, mp, 0), (mz_h, mz, 0), (mat_h, mat, 0)]
    ):
        d = dst.at[0:LAYERS] if k else dst
        inner = pltpu.make_async_copy(src.at[:, 0:RI], d.at[:, 0:RI], in_sem.at[2 * n])
        outer = pltpu.make_async_copy(src.at[:, RI:NR], d.at[:, RI:NR], in_sem.at[2 * n + 1])
        loads.append((inner, outer))
    for inner, _ in loads:
        inner.start()
    for _, outer in loads:
        outer.start()

    barrier = pltpu.get_barrier_semaphore()
    for d in (sib, dev_z1, dev_z3, dev_y, nxt, prv):
        pl.semaphore_signal(barrier, inc=1, device_id={"phi": d}, device_id_type=MESH)
    for d in (up, down):
        pl.semaphore_signal(barrier, inc=1, device_id={"gz": d}, device_id_type=MESH)

    row = lax.broadcasted_iota(jnp.int32, (NR, 128), 0)
    rn = inner_radius + row.astype(F32)
    rc = rn + 0.5
    inv_rn = 1.0 / rn
    inv_rc = 1.0 / rc
    first = row == 0
    coef[C_DT_RN] = (dt / dphi) * inv_rn
    coef[C_UP] = dt * (rn + 1.0) * inv_rc
    coef[C_HERE] = dt * rn * inv_rc
    coef[C_DT_RC] = (dt / dphi) * inv_rc
    coef[C_RC] = (1.0 / dphi) * inv_rc
    coef[C_KEEP_PREV] = jnp.where(first, 0.0, 1.0)
    coef[C_P] = rc * inv_rn
    coef[C_Q] = jnp.where(first, 0.0, (rc - 1.0) * inv_rn)
    coef[C_RN] = (1.0 / dphi) * inv_rn

    for number in range(NMAT):
        eps = jnp.full((8, 128), perm[number], F32)
        sig = jnp.full((8, 128), cond[number], F32)
        loss = sig * dt / (2.0 * eps)
        ktab[0, number] = (1.0 - loss) / (1.0 + loss)
        ktab[1, number] = dt / (eps * (1.0 + loss))

    mode = lax.broadcasted_iota(jnp.int32, (NF, 128), 1)
    wrow = lax.broadcasted_iota(jnp.int32, (NF, 128), 0)
    cuts = jnp.zeros((NF, 128), jnp.int32)
    for number in range(NF):
        cuts = jnp.where(wrow == number, cut[number], cuts)
    weight = jnp.where(mode == 0, 1.0 / NPHI, 2.0 / NPHI)
    weight = jnp.where(mode <= cuts, weight, 0.0)
    wts[:, 0:128] = weight
    wts[:, 128:256] = weight

    for place, who in ((0, phi), (1, sib)):
        pc = phase[0, pl.ds(who, 1), :]
        ps = phase[1, pl.ds(who, 1), :]
        cosb = base[0] * pc - base[1] * ps
        sinb = base[1] * pc + base[0] * ps
        dcos = base[2] * pc - base[3] * ps
        dsin = base[3] * pc + base[2] * ps
        lo_row = place * 128
        for part, m in ((0, cosb), (1, sinb)):
            h, l = split(m)
            fwd[0, lo_row : lo_row + 128, part * 128 : part * 128 + 128] = h
            fwd[1, lo_row : lo_row + 128, part * 128 : part * 128 + 128] = l
        for kind, (mc, ms) in ((0, (cosb, sinb)), (1, (dcos, dsin))):
            col = kind * 256 + place * 128
            for part, m in ((0, mc), (1, ms)):
                h, l = split(m.T)
                inv[0, part * 128 : part * 128 + 128, col : col + 128] = h
                inv[1, part * 128 : part * 128 + 128, col : col + 128] = l

    def clear(k, _):
        eh[k, NR : NR + 8] = jnp.zeros((8, 128), F32)
        ea[k, NR : NR + 8] = jnp.zeros((8, 128), F32)
        return 0

    lax.fori_loop(0, LAYERS, clear, 0)
    p1s[...] = jnp.zeros_like(p1s)
    p2s[...] = jnp.zeros_like(p2s)

    pl.semaphore_wait(barrier, 8)

    def border(src, dst, n, dev):
        return pltpu.make_async_remote_copy(
            src_ref=src, dst_ref=dst, send_sem=bsend.at[n], recv_sem=brecv.at[n],
            device_id=dev, device_id_type=MESH,
        )

    b_er = border(er_h.at[0], er.at[LAYERS], B_ER, {"gz": down})
    b_ea = border(ea_h.at[0], ea.at[LAYERS, 0:NR], B_EA, {"gz": down})
    b_p1i = border(p1s.at[0:NF], p1r.at[0:NF], B_P1I, {"phi": prv})
    b_p1o = border(p1s.at[NF:NR], p1r.at[NF:NR], B_P1O, {"phi": prv})
    b_p2 = border(p2s, p2r, B_P2, {"phi": nxt})
    b_hi = border(hf.at[LAYERS, 0:2], hf.at[0, 0:2], B_HI, {"gz": up})
    b_ho = border(ho.at[LAYERS, :, 8:104], ho.at[0, :, 8:104], B_HO, {"gz": up})

    b_er.start()
    b_ea.start()

    def pack_first(lo, hi):
        def body(k, _):
            a = pltpu.roll(eh[k, lo:hi], k, 1)
            b = pltpu.roll(er[k, lo:hi], HALO_R + k, 1)
            p1s[lo:hi] = jnp.where(lane == k, a, jnp.where(lane == HALO_R + k, b, p1s[lo:hi]))
            return 0

        lax.fori_loop(0, LAYERS, body, 0)

    loads[0][0].wait()
    loads[1][0].wait()
    pack_first(0, NF)
    b_p1i.start()
    for n in range(2, 6):
        loads[n][0].wait()
    b_er.wait_recv()
    b_ea.wait_recv()
    above = jnp.where(gz == 7, 0.0, 1.0)
    er[LAYERS] = er[LAYERS] * above
    ea[LAYERS, 0:NR] = ea[LAYERS, 0:NR] * above
    b_p1i.wait_recv()

    def magnetic(k, lo, hi):
        def ahead(x, n):
            return jnp.where(lane == 127, pltpu.roll(p1r[lo:hi], 127 - n, 1), pltpu.roll(x, 127, 1)) - x

        e_h = eh[k, lo:hi]
        e_r = er[k, lo:hi]
        e_a = ea[k, lo:hi]
        hr = mr[k, lo:hi] - coef[C_DT_RN, lo:hi] * ahead(e_h, k) + dt * (ea[k + 1, lo:hi] - e_a)
        hp = mp[k, lo:hi] - dt * ((er[k + 1, lo:hi] - e_r) - (eh[k, lo + 1 : hi + 1] - e_h))
        hz = (
            mz[k, lo:hi]
            - (coef[C_UP, lo:hi] * ea[k, lo + 1 : hi + 1] - coef[C_HERE, lo:hi] * e_a)
            + coef[C_DT_RC, lo:hi] * ahead(e_r, HALO_R + k)
        )
        return hr, hp, hz

    def factors(k, lo, hi):
        kind = mat[k, lo:hi]
        keep = jnp.broadcast_to(ktab[0, 0, 0:1], kind.shape)
        drive = jnp.broadcast_to(ktab[1, 0, 0:1], kind.shape)
        for number in range(1, NMAT):
            here = kind == number
            keep = jnp.where(here, ktab[0, number, 0:1], keep)
            drive = jnp.where(here, ktab[1, number, 0:1], drive)
        return keep, drive

    def move(f, c, stage, src, dst, dev):
        n = f * CHUNKS + c
        return pltpu.make_async_remote_copy(
            src_ref=src, dst_ref=dst, send_sem=send.at[n, stage], recv_sem=recv.at[n, stage],
            device_id={"phi": dev}, device_id_type=MESH,
        )

    def d_a(f, c):
        return [move(f, c, ST_A, g.at[f, pl.ds(PER_CHUNK * c + HALF * (1 - q), HALF)], ra.at[f, c], sib)]

    def d_1(f, c):
        return [
            move(f, c, ST_1A, s.at[f, c, pl.ds(2 * (1 - f1), 2), :, 0:16], r1.at[f, c, 0], dev_z1),
            move(f, c, ST_1B, s.at[f, c, pl.ds(2 * (1 - g1), 2), :, 16:32], r1.at[f, c, 1], dev_z3),
        ]

    def d_2(f, c):
        return [
            move(f, c, ST_2A, s.at[f, c, 2 * f1 + 1 - f2, :, 0:16], r2.at[f, c, 0], dev_z3),
            move(f, c, ST_2B, s.at[f, c, 2 * g1 + 1 - g2, :, 16:32], r2.at[f, c, 1], dev_z1),
        ]

    def d_c(f, c):
        return [move(f, c, ST_C, u.at[f, c], rc_buf.at[f, c], dev_y)]

    def d_3(f, c):
        a = t.at[f, c, 2 * f1 + f2, :, 0:16]
        b = t.at[f, c, 2 * g1 + g2, :, 16:32]
        return [move(f, c, ST_3A, a, a, dev_z3), move(f, c, ST_3B, b, b, dev_z1)]

    def d_4(f, c):
        a = t.at[f, c, pl.ds(2 * f1, 2), :, 0:16]
        b = t.at[f, c, pl.ds(2 * g1, 2), :, 16:32]
        return [move(f, c, ST_4A, a, a, dev_z1), move(f, c, ST_4B, b, b, dev_z3)]

    def d_z(f, c):
        start = PER_CHUNK * c + HALF * q
        if f == 0:
            return [move(f, c, ST_Z, v.at[c], hf.at[pl.ds(1 + start, HALF)], sib)]
        return [
            move(f, c, ST_Z + n, v2.at[c, n], o.at[pl.ds(start, HALF), 0:NF], sib)
            for n, o in enumerate((o_er, o_ea, o_eh))
        ]

    def go(copies):
        for d in copies:
            d.start()

    def arrived(copies):
        for d in copies:
            d.wait_recv()

    def stage_1(f, c):
        arrived(d_a(f, c))
        own = g[f, pl.ds(PER_CHUNK * c + HALF * q, HALF)].reshape(HALF * 96, 128)
        x = jnp.concatenate([own, ra[f, c].reshape(HALF * 96, 128)], axis=1)
        s[f, c] = dot3(x, fwd[0], fwd[1]).reshape(HALF, 3, NF, 256)
        go(d_1(f, c))

    def stage_2(f, c):
        arrived(d_1(f, c))
        s[f, c, pl.ds(2 * f1, 2), :, 0:16] = s[f, c, pl.ds(2 * f1, 2), :, 0:16] + r1[f, c, 0]
        s[f, c, pl.ds(2 * g1, 2), :, 16:32] = s[f, c, pl.ds(2 * g1, 2), :, 16:32] + r1[f, c, 1]
        go(d_2(f, c))

    def stage_3(f, c):
        arrived(d_2(f, c))
        u[f, c, 0] = s[f, c, 2 * f1 + f2, :, 0:16] + r2[f, c, 0]
        u[f, c, 1] = s[f, c, 2 * g1 + g2, :, 16:32] + r2[f, c, 1]
        go(d_c(f, c))

    def stage_4(f, c):
        arrived(d_c(f, c))
        t[f, c, 2 * f1 + f2, :, 0:16] = (u[f, c, 0] + rc_buf[f, c, 0]) * wts[0:16][None]
        t[f, c, 2 * g1 + g2, :, 16:32] = (u[f, c, 1] + rc_buf[f, c, 1]) * wts[16:32][None]
        go(d_3(f, c))

    def stage_5(f, c):
        arrived(d_3(f, c))
        go(d_4(f, c))

    def stage_6(f, c):
        arrived(d_4(f, c))
        x = t[f, c].reshape(HALF * 96, 256)
        start = PER_CHUNK * c + HALF * q
        value = dot3(x, inv[0, :, 0:256], inv[1, :, 0:256]).reshape(HALF, 3, NF, 256)
        if f == 0:
            slope = dot3(x, inv[0, :, 256:512], inv[1, :, 256:512]).reshape(HALF, 3, NF, 256)
            v[c, :, 0:3] = value[..., 128:256]
            v[c, :, 3] = slope[:, 0, :, 128:256]
            v[c, :, 4] = slope[:, 2, :, 128:256]
            go(d_z(f, c))
            hf[pl.ds(1 + start, HALF), 0:3] = value[..., 0:128]
            hf[pl.ds(1 + start, HALF), 3] = slope[:, 0, :, 0:128]
            hf[pl.ds(1 + start, HALF), 4] = slope[:, 2, :, 0:128]
        else:
            for n in range(3):
                v2[c, n] = value[:, n, :, 128:256]
            go(d_z(f, c))
            for n, o in enumerate((o_er, o_ea, o_eh)):
                o[pl.ds(start, HALF), 0:NF] = value[:, n, :, 0:128]

    def each(stage, f):
        def body(c, _):
            stage(f, c)
            return 0

        lax.fori_loop(0, CHUNKS, body, 0)

    def begin_h(f, c):
        def body(k, _):
            hr, hp, hz = magnetic(k, 0, NF)
            g[0, k, 0] = hr
            g[0, k, 1] = hp
            g[0, k, 2] = hz
            return 0

        lax.fori_loop(PER_CHUNK * c, PER_CHUNK * c + PER_CHUNK, body, 0)
        go(d_a(0, c))

    each(begin_h, 0)
    for n in range(7):
        loads[n][1].wait()
    loads[6][0].wait()
    pack_first(NF, NR)
    b_p1o.start()
    each(stage_1, 0)

    def inner_factors(k, _):
        keep, drive = factors(k, 0, NF)
        ki[k, 0] = keep
        ki[k, 1] = drive
        return 0

    lax.fori_loop(0, LAYERS, inner_factors, 0)
    b_p1o.wait_recv()
    each(stage_2, 0)

    def outer_h(k, _):
        hr, hp, hz = magnetic(k, NF, NR)
        ho[k + 1, 0, 8:104] = hr
        ho[k + 1, 1, 8:104] = hp
        o_hz[k, NF:NR] = hz
        p2s[...] = jnp.where(
            lane == k,
            pltpu.roll(hr, k + 1, 1),
            jnp.where(lane == HALO_R + k, pltpu.roll(hz, HALO_R + k + 1, 1), p2s[...]),
        )
        return 0

    each(stage_3, 0)
    lax.fori_loop(0, LAYERS, outer_h, 0)
    b_p2.start()
    b_ho.start()
    each(stage_4, 0)
    each(stage_5, 0)
    each(stage_6, 0)

    below = jnp.where(gz == 0, 0.0, 1.0)

    def electric_inner(k, _):
        hr, hp, hz = hf[k + 1, 0], hf[k + 1, 1], hf[k + 1, 2]
        keep, drive = ki[k, 0], ki[k, 1]
        back = pltpu.roll(hp, 1, 0)
        g[1, k, 0] = keep * er[k, 0:NF] + drive * (coef[C_RC, 0:NF] * hf[k + 1, 4] - (hp - hf[k, 1]))
        g[1, k, 1] = keep * ea[k, 0:NF] + drive * ((hr - hf[k, 0]) - (hp - coef[C_KEEP_PREV, 0:NF] * back))
        g[1, k, 2] = keep * eh[k, 0:NF] + drive * (
            coef[C_P, 0:NF] * hp - coef[C_Q, 0:NF] * back - coef[C_RN, 0:NF] * hf[k + 1, 3]
        )
        return 0

    def begin_e(c):
        lax.fori_loop(PER_CHUNK * c, PER_CHUNK * c + PER_CHUNK, electric_inner, 0)
        go(d_a(1, c))

    for c in range(CHUNKS):
        arrived(d_z(0, c))
    b_hi.start()
    begin_e(1)
    begin_e(2)
    b_hi.wait_recv()
    hf[0, 0:2] = hf[0, 0:2] * below
    begin_e(0)

    def in_order(stage, f):
        def body(n, _):
            stage(f, (n + 1) % CHUNKS)
            return 0

        lax.fori_loop(0, CHUNKS, body, 0)

    in_order(stage_1, 1)

    def finish_h(k, _):
        o_hr[k, 0:NF] = hf[k + 1, 0]
        o_hp[k, 0:NF] = hf[k + 1, 1]
        o_hz[k, 0:NF] = hf[k + 1, 2]
        ho[k + 1, 1, 0:8] = hf[k + 1, 1, 24:32]
        return 0

    lax.fori_loop(0, LAYERS, finish_h, 0)
    in_order(stage_2, 1)
    b_p2.wait_recv()
    b_ho.wait_recv()
    ho[0, :, 8:104] = ho[0, :, 8:104] * below

    def outer_e(k, _):
        hr, hp = ho[k + 1, 0, 8:104], ho[k + 1, 1, 8:104]
        hz = o_hz[k, NF:NR]
        back = ho[k + 1, 1, 7:103]
        keep, drive = factors(k, NF, NR)

        def behind(x, n):
            return x - jnp.where(lane == 0, pltpu.roll(p2r[...], (128 - n) % 128, 1), pltpu.roll(x, 1, 1))

        o_hr[k, NF:NR] = hr
        o_hp[k, NF:NR] = hp
        o_er[k, NF:NR] = keep * er[k, NF:NR] + drive * (
            coef[C_RC, NF:NR] * behind(hz, HALO_R + k) - (hp - ho[k, 1, 8:104])
        )
        o_ea[k, NF:NR] = keep * ea[k, NF:NR] + drive * ((hr - ho[k, 0, 8:104]) - (hp - back))
        o_eh[k, NF:NR] = keep * eh[k, NF:NR] + drive * (
            coef[C_P, NF:NR] * hp - coef[C_Q, NF:NR] * back - coef[C_RN, NF:NR] * behind(hr, k)
        )
        return 0

    in_order(stage_3, 1)
    lax.fori_loop(0, LAYERS, outer_e, 0)
    in_order(stage_4, 1)
    in_order(stage_5, 1)
    in_order(stage_6, 1)
    for c in range(CHUNKS):
        arrived(d_z(1, c))

    def drained(c, _):
        for f in range(2):
            for kind in (d_a, d_1, d_2, d_c, d_3, d_4, d_z):
                for d in kind(f, c):
                    d.wait_send()
        return 0

    lax.fori_loop(0, CHUNKS, drained, 0)
    for d in (b_er, b_ea, b_p1i, b_p1o, b_p2, b_hi, b_ho):
        d.wait_send()


def local(er, ea, eh, mr, mp, mz, material, permittivity, conductivity, mode_cutoff):
    base, phase = basis_tables()
    field = (LAYERS, NR, WIDTH)
    anywhere = pl.BlockSpec(memory_space=pl.ANY)
    smem = pl.BlockSpec(memory_space=pltpu.SMEM)
    vmem = pl.BlockSpec(memory_space=pltpu.VMEM)

    def scratch(*shape, dtype=F32):
        return pltpu.VMEM(shape, dtype)

    call = pl.pallas_call(
        kernel,
        out_shape=tuple(pltpu.VMEM(field, F32) for _ in range(6)),
        in_specs=[anywhere] * 7 + [smem] * 3 + [vmem] * 2,
        out_specs=tuple([vmem] * 6),
        scratch_shapes=[
            scratch(LAYERS + 1, NR, WIDTH),
            scratch(LAYERS + 1, NR + 8, WIDTH),
            scratch(LAYERS, NR + 8, WIDTH),
            scratch(*field),
            scratch(*field),
            scratch(*field),
            scratch(*field, dtype=jnp.int32),
            scratch(9, NR, 128),
            scratch(2, NMAT, 8, 128),
            scratch(NF, 256),
            scratch(2, 256, 256, dtype=BF16),
            scratch(2, 256, 512, dtype=BF16),
            scratch(NR, 128),
            scratch(NR, 128),
            scratch(NR - NF, 128),
            scratch(NR - NF, 128),
            scratch(2, LAYERS, 3, NF, 128),
            scratch(2, CHUNKS, HALF, 3, NF, 128),
            scratch(2, CHUNKS, HALF, 3, NF, 256),
            scratch(2, CHUNKS, 2, 2, 3, 16, 256),
            scratch(2, CHUNKS, 2, 3, 16, 256),
            scratch(2, CHUNKS, 2, 3, 16, 256),
            scratch(2, CHUNKS, 2, 3, 16, 256),
            scratch(2, CHUNKS, HALF, 3, NF, 256),
            scratch(CHUNKS, HALF, 5, NF, 128),
            scratch(CHUNKS, 3, HALF, NF, 128),
            scratch(LAYERS + 1, 5, NF, 128),
            scratch(LAYERS + 1, 2, 104, 128),
            scratch(LAYERS, 2, NF, 128),
            pltpu.SemaphoreType.DMA((14,)),
            pltpu.SemaphoreType.DMA((2 * CHUNKS, NSTAGE)),
            pltpu.SemaphoreType.DMA((2 * CHUNKS, NSTAGE)),
            pltpu.SemaphoreType.DMA((7,)),
            pltpu.SemaphoreType.DMA((7,)),
        ],
        compiler_params=pltpu.CompilerParams(
            collective_id=0, has_side_effects=True, vmem_limit_bytes=44 * 1024 * 1024
        ),
        name="yee_step",
    )
    return call(
        er, ea, eh, mr, mp, mz, material, permittivity, conductivity, mode_cutoff,
        jnp.asarray(base), jnp.asarray(phase),
    )


def solution(mesh):
    field = P("gz", None, "phi")
    return jax.shard_map(
        local,
        mesh=mesh,
        in_specs=(field,) * 7 + (P(),) * 3,
        out_specs=(field,) * 6,
        check_vma=False,
    )
```

time: 431 us -> 98.5 us (0.23)
  waiting for transfers between devices: 246 us -> 0 us
  Pallas kernels: 0 us -> 87.1 us
  other arithmetic: 71.7 us -> 0 us
  matrix products: 40.8 us -> 0 us
  local copies, waits for them, and re-layouts: 39.9 us -> 10.5 us
  starting transfers between devices: 17.3 us -> 0 us
  between operations: 14.7 us -> 0.66 us
    all_gather x2 -> x0, waiting for transfers between devices: 246 us -> none  [cycle_filter(): portion = lax.all_gather(stacked, 'phi', axis=3, tiled=True)]
    pallas_call x0 -> x1, Pallas kernels: none -> 87.1 us  [local(): call(er, ea, eh, mr, mp, mz, material, permittivity, conductivity, mode_c...]
    add x6 -> x0, other arithmetic: 44.1 us -> none  [the longest x1 15.9 us: local(): keep_factor * electric_azimuth]
    dot_general x4 -> x0, matrix products: 40.8 us -> none  [the longest x2 36.8 us: transform(): jnp.dot(flat, basis, precision=lax.Precision.HIGHEST, preferred_element_t...]
    slice x17 -> x0, local copies, waits for them, and re-layouts: 17.2 us -> none  [the longest x2 3.55 us: filter_three(): second[:, NF:]]
    ppermute x8 -> x0, starting transfers between devices: 17.1 us -> none  [the longest x4 9.37 us: shifted_2(): return lax.ppermute(block, axis, route)]
    concatenate x9 -> x0, other arithmetic: 10.1 us -> none  [the longest x3 3.78 us: filter_three(): jnp.concatenate([filtered[0], first[:, NF:]], axis=1)]
    broadcast_in_dim x4 -> x0, local copies, waits for them, and re-layouts: 8.06 us -> none  [the longest x2 4.75 us: behind_azimuth(): border[:, :, None]]
  transfers between devices with their start and end apart: 10 -> 0, of which waited for: 2 -> 0; matrix products, arithmetic and copies ran while one was open for 11% -> 0% of each run, Pallas kernels for 0% -> 0%
where the time goes in v1:
time: 98.5 us; the launch traced here: 98.3 us
  Pallas kernels  87.1 us (88%)
  local copies, waits for them, and re-layouts  10.5 us (11%)
    pallas_call x1, Pallas kernels, local(): call(er, ea, eh, mr, mp, mz, material, permittivity, conductivity, mode_c...  87.1 us
    unnamed x16, local copies, waits for them, and re-layouts  10.5 us

profile of v1, /device:TPU:1, one launch (start us, length us, event | category | flops | bytes accessed | tf_op | source)
XLA Modules:
  0.0 98.3 jit_solution(7964709005279395906)
XLA Ops:
  0.6 0.0 copy-start
  0.6 0.9 copy-done
  1.6 0.0 copy-start.1
  1.6 0.7 copy-done.1
  2.3 0.0 copy-start.2
  2.3 0.7 copy-done.2
  3.0 0.0 copy-start.3
  3.0 0.7 copy-done.3
  3.6 0.0 copy-start.4
  3.6 0.7 copy-done.4
  4.3 87.1 %yee_step.1 = (f32[24,128,128]{2,1,0:T(8,128)S(1)}, f32[24,128,128]{2,1,0:T(8,128)S(1)}, f32[24,128,128]{2,1,0:T(8,128)S(1)}, f32[24,128,128]{2,1,0:T(8,128)S(1)...) custom-call(f32[24,128,128]{2,1,0:T(8,128)} %er_h.1, f32[24,128,128]{2,1,0:T(8,128)} %ea_h.1, ...), custom_call_target="tpu_custom_call" | custom-call | tf_op jit(solution)/shard_map/yee_step/pallas_call | solution.py:544
  91.4 1.1 %copy.24 = f32[24,128,128]{2,1,0:T(8,128)} copy(f32[24,128,128]{2,1,0:T(8,128)S(1)} %get-tuple-element.6) | data formatting | bytes 3145728
  92.6 1.1 %copy.25 = f32[24,128,128]{2,1,0:T(8,128)} copy(f32[24,128,128]{2,1,0:T(8,128)S(1)} %get-tuple-element.7) | data formatting | bytes 3145728
  93.7 1.1 %copy.26 = f32[24,128,128]{2,1,0:T(8,128)} copy(f32[24,128,128]{2,1,0:T(8,128)S(1)} %get-tuple-element.8) | data formatting | bytes 3145728
  94.9 1.1 %copy.27 = f32[24,128,128]{2,1,0:T(8,128)} copy(f32[24,128,128]{2,1,0:T(8,128)S(1)} %get-tuple-element.9) | data formatting | bytes 3145728
  96.0 1.1 %copy.28 = f32[24,128,128]{2,1,0:T(8,128)} copy(f32[24,128,128]{2,1,0:T(8,128)S(1)} %get-tuple-element.10) | data formatting | bytes 3145728
  97.1 1.1 %copy.29 = f32[24,128,128]{2,1,0:T(8,128)} copy(f32[24,128,128]{2,1,0:T(8,128)S(1)} %get-tuple-element.11) | data formatting | bytes 3145728
Async XLA Ops:
  0.6 1.0 copy-start
  1.6 0.7 copy-start.1
  2.3 0.7 copy-start.2
  3.0 0.7 copy-start.3
  3.6 0.7 copy-start.4

commit v2 on v1

v2 whole, which is shorter than its diff:
```python
import math

import jax
import jax.numpy as jnp
import numpy as np
from jax import lax
from jax.experimental import pallas as pl
from jax.experimental.pallas import tpu as pltpu
from jax.sharding import PartitionSpec as P

KMAX = 128
NF = 32
NMAT = 8
NPHI = 2048
NR = 128
OUT = NR - NF
LAYERS = 24
WIDTH = 128
CHUNKS = 3
PER_CHUNK = 8
PAIRS = LAYERS // 2
HALO_R = 32

inner_radius = 64.0
dt = 0.2
dphi = 2.0 * math.pi / NPHI
MESH = pl.DeviceIdType.MESH
F32 = jnp.float32
BF16 = jnp.bfloat16

C_DT_RN, C_UP, C_HERE, C_DT_RC, C_RC, C_KEEP_PREV, C_P, C_Q, C_RN = range(9)
ST_Q, ST_2, ST_C, ST_3, ST_Z = 0, 6, 8, 9, 11
NSTAGE = 17
B_P1I, B_P1O, B_ER, B_EA, B_P2, B_HI, B_HI2, B_HO = range(8)


def basis_tables():
    j = np.arange(WIDTH + 8, dtype=np.float64)[:, None]
    j[WIDTH:] = -1.0
    m = np.arange(KMAX, dtype=np.float64)[None, :]
    a = 2.0 * np.pi * j * m / NPHI
    base = np.stack([np.cos(a), np.sin(a)])
    turn = 2.0 * np.pi * ((np.arange(16)[:, None] * WIDTH * np.arange(KMAX)[None, :]) % NPHI) / NPHI
    phase = np.stack([np.cos(turn), np.sin(turn)])
    return base.astype(np.float32), phase.astype(np.float32)


def split(x):
    hi = x.astype(BF16)
    lo = (x - hi.astype(F32)).astype(BF16)
    return hi, lo


def dot3(x, b_hi, b_lo, dims):
    hi, lo = split(x)

    def dot(a, b):
        return lax.dot_general(a, b, (dims, ((), ())), preferred_element_type=F32)

    return dot(hi, b_hi) + dot(lo, b_hi) + dot(hi, b_lo)


def kernel(
    er_h, ea_h, eh_h, mr_h, mp_h, mz_h, mat_h, perm_h, cond_h, cut_h, base_h, phase_h,
    ho, o_hz, o_er, o_ea, o_eh, rz1, rz2,
    er, ea, eh, mr, mp, mz, mat,
    perm, cond, cut, base, phase,
    coef, ktab, wts, tab,
    p1s, p1r, p2s, p2r,
    g, rq, s, r2, u, ru, t, v1, v2, ki,
    in_sem, send, recv, bsend, brecv,
):
    phi = lax.axis_index("phi")
    gz = lax.axis_index("gz")
    q = phi % 2
    z = (phi // 2) % 4
    hi_bit = z // 2
    low_bit = z % 2
    gray = (hi_bit + low_bit) % 2
    sib = phi + 1 - 2 * q
    half = (phi // 8) * 8
    dev_z1 = half + (z + 1 - 2 * low_bit) * 2 + q
    dev_z3 = half + (3 - z) * 2 + q
    sib_z1 = dev_z1 + 1 - 2 * q
    sib_z3 = dev_z3 + 1 - 2 * q
    dev_y = (phi + 8) % 16
    nxt = (phi + 1) % 16
    prv = (phi + 15) % 16
    up = (gz + 1) % 8
    down = (gz + 7) % 8
    first_bit = (gray, hi_bit)
    second_bit = (hi_bit, gray)
    first_dev = ((dev_z1, sib_z1), (dev_z3, sib_z3))
    second_dev = (dev_z3, dev_z1)
    pair = tuple(2 * q + b for b in first_bit)

    lane = lax.broadcasted_iota(jnp.int32, (1, 128), 1)

    small = [
        pltpu.make_async_copy(src, dst, in_sem.at[14 + n])
        for n, (src, dst) in enumerate(
            [(base_h, base), (phase_h, phase), (perm_h, perm), (cond_h, cond), (cut_h, cut)]
        )
    ]
    loads = []
    RI = 40
    for n, (src, dst) in enumerate(
        [(eh_h, eh), (er_h, er.at[0:LAYERS]), (ea_h, ea.at[0:LAYERS]), (mr_h, mr), (mp_h, mp), (mz_h, mz), (mat_h, mat)]
    ):
        inner = pltpu.make_async_copy(src.at[:, 0:RI], dst.at[:, 0:RI], in_sem.at[2 * n])
        outer = pltpu.make_async_copy(src.at[:, RI:NR], dst.at[:, RI:NR], in_sem.at[2 * n + 1])
        loads.append((inner, outer))

    barrier = pltpu.get_barrier_semaphore()
    for d in (sib, dev_z1, sib_z1, dev_z3, sib_z3, dev_y, nxt, prv):
        pl.semaphore_signal(barrier, inc=1, device_id={"phi": d}, device_id_type=MESH)
    for d in (up, down):
        pl.semaphore_signal(barrier, inc=1, device_id={"gz": d}, device_id_type=MESH)
    for inner, _ in loads[0:2]:
        inner.start()
    for d in small:
        d.start()
    for inner, _ in loads[2:]:
        inner.start()
    for _, outer in loads:
        outer.start()

    p1s[...] = jnp.zeros_like(p1s)
    p2s[...] = jnp.zeros_like(p2s)

    def pack_first(lo, hi):
        def body(k, _):
            a = pltpu.roll(eh[k, lo:hi], k, 1)
            b = pltpu.roll(er[k, lo:hi], HALO_R + k, 1)
            p1s[lo:hi] = jnp.where(lane == k, a, jnp.where(lane == HALO_R + k, b, p1s[lo:hi]))
            return 0

        lax.fori_loop(0, LAYERS, body, 0)

    loads[0][0].wait()
    loads[1][0].wait()
    pack_first(0, NF)

    pl.semaphore_wait(barrier, 10)

    def border(src, dst, n, dev):
        return pltpu.make_async_remote_copy(
            src_ref=src, dst_ref=dst, send_sem=bsend.at[n], recv_sem=brecv.at[n],
            device_id=dev, device_id_type=MESH,
        )

    b_er = border(er_h.at[0], er.at[LAYERS], B_ER, {"gz": down})
    b_ea = border(ea_h.at[0], ea.at[LAYERS, 0:NR], B_EA, {"gz": down})
    b_p1i = border(p1s.at[0:NF], p1r.at[0:NF], B_P1I, {"phi": prv})
    b_p1o = border(p1s.at[NF:NR], p1r.at[NF:NR], B_P1O, {"phi": prv})
    b_p2 = border(p2s, p2r, B_P2, {"phi": nxt})
    b_hi = border(rz1.at[0, PAIRS, 3:5], rz1.at[0, 0, 3:5], B_HI, {"gz": up})
    b_hi2 = border(rz1.at[1, PAIRS, 3:5], rz1.at[1, 0, 3:5], B_HI2, {"gz": up})
    b_ho = border(ho.at[LAYERS, :, 8:104], ho.at[0, :, 8:104], B_HO, {"gz": up})

    b_p1i.start()
    b_er.start()
    b_ea.start()

    def clear(k, _):
        eh[k, NR : NR + 8] = jnp.zeros((8, 128), F32)
        ea[k, NR : NR + 8] = jnp.zeros((8, 128), F32)
        return 0

    lax.fori_loop(0, LAYERS, clear, 0)
    row = lax.broadcasted_iota(jnp.int32, (NR, 128), 0)
    rn = inner_radius + row.astype(F32)
    rc = rn + 0.5
    inv_rn = 1.0 / rn
    inv_rc = 1.0 / rc
    first = row == 0
    coef[C_DT_RN] = (dt / dphi) * inv_rn
    coef[C_UP] = dt * (rn + 1.0) * inv_rc
    coef[C_HERE] = dt * rn * inv_rc
    coef[C_DT_RC] = (dt / dphi) * inv_rc
    coef[C_RC] = (1.0 / dphi) * inv_rc
    coef[C_KEEP_PREV] = jnp.where(first, 0.0, 1.0)
    coef[C_P] = rc * inv_rn
    coef[C_Q] = jnp.where(first, 0.0, (rc - 1.0) * inv_rn)
    coef[C_RN] = (1.0 / dphi) * inv_rn
    for d in small:
        d.wait()

    for kind in range(2):
        for place, who in enumerate((phi, sib) + first_dev[kind]):
            pc = phase[0, pl.ds(who, 1), :]
            ps = phase[1, pl.ds(who, 1), :]
            if kind == 1 and place < 2:
                tab[:, 1, place * 128 : place * 128 + 128] = tab[:, 0, place * 128 : place * 128 + 128]
            else:
                for part, m in ((0, base[0, 0:128] * pc - base[1, 0:128] * ps), (1, base[1, 0:128] * pc + base[0, 0:128] * ps)):
                    h, l = split(m)
                    tab[0, kind, place * 128 : place * 128 + 128, part * 128 : part * 128 + 128] = h
                    tab[1, kind, place * 128 : place * 128 + 128, part * 128 : part * 128 + 128] = l
            bc, bs = base[0, 128:129], base[1, 128:129]
            lo_row = 512 + place * 32
            for part, m in ((0, bc * pc - bs * ps), (1, bs * pc + bc * ps)):
                h, l = split(jnp.broadcast_to(m, (32, 128)))
                tab[0, kind, lo_row : lo_row + 32, part * 128 : part * 128 + 128] = h
                tab[1, kind, lo_row : lo_row + 32, part * 128 : part * 128 + 128] = l

    for n in range(2, 6):
        loads[n][0].wait()
    b_er.wait_recv()
    b_ea.wait_recv()
    above = jnp.where(gz == 7, 0.0, 1.0)
    er[LAYERS] = er[LAYERS] * above
    ea[LAYERS, 0:NR] = ea[LAYERS, 0:NR] * above
    b_p1i.wait_recv()

    def magnetic(k, lo, hi):
        def ahead(x, n):
            return jnp.where(lane == 127, pltpu.roll(p1r[lo:hi], 127 - n, 1), pltpu.roll(x, 127, 1)) - x

        e_h = eh[k, lo:hi]
        e_r = er[k, lo:hi]
        e_a = ea[k, lo:hi]
        hr = mr[k, lo:hi] - coef[C_DT_RN, lo:hi] * ahead(e_h, k) + dt * (ea[k + 1, lo:hi] - e_a)
        hp = mp[k, lo:hi] - dt * ((er[k + 1, lo:hi] - e_r) - (eh[k, lo + 1 : hi + 1] - e_h))
        hz = (
            mz[k, lo:hi]
            - (coef[C_UP, lo:hi] * ea[k, lo + 1 : hi + 1] - coef[C_HERE, lo:hi] * e_a)
            + coef[C_DT_RC, lo:hi] * ahead(e_r, HALO_R + k)
        )
        return hr, hp, hz

    def factors(k, lo, hi):
        kind = mat[k, lo:hi]
        keep = jnp.broadcast_to(ktab[0, 0, 0:1], kind.shape)
        drive = jnp.broadcast_to(ktab[1, 0, 0:1], kind.shape)
        for number in range(1, NMAT):
            here = kind == number
            keep = jnp.where(here, ktab[0, number, 0:1], keep)
            drive = jnp.where(here, ktab[1, number, 0:1], drive)
        return keep, drive

    def move(f, c, stage, src, dst, dev):
        n = f * CHUNKS + c
        return pltpu.make_async_remote_copy(
            src_ref=src, dst_ref=dst, send_sem=send.at[n, stage], recv_sem=recv.at[n, stage],
            device_id={"phi": dev}, device_id_type=MESH,
        )

    def d_q(f, c):
        out = []
        for a in range(2):
            b = first_bit[a]
            pairs = (2 * q + 1 - b, 2 * (1 - q) + 1 - b, 2 * (1 - q) + b)
            devs = first_dev[a] + (sib,)
            slots = (1, 2, 0)
            for n in range(3):
                src = g.at[f, a, pl.ds(PER_CHUNK * c + 2 * pairs[n], 2)]
                out.append(move(f, c, ST_Q + 3 * a + n, src, rq.at[f, c, a, slots[n]], devs[n]))
        return out

    def d_2(f, c, sets=(0, 1)):
        return [
            move(f, c, ST_2 + a, s.at[f, c, a, 1 - second_bit[a]], r2.at[f, c, a], second_dev[a])
            for a in sets
        ]

    def d_c(f, c):
        return [move(f, c, ST_C, u.at[f, c], ru.at[f, c], dev_y)]

    def d_3(f, c):
        out = []
        for a in range(2):
            own = t.at[f, c, a, second_bit[a]]
            out.append(move(f, c, ST_3 + a, own, own, second_dev[a]))
        return out

    def d_z(f, c, sets=(0, 1)):
        out = []
        for a in sets:
            devs = first_dev[a] + (sib,)
            slots = (1, 2, 0)
            for n in range(3):
                if f == 0:
                    src, dst = v1.at[c, a, slots[n]], rz1.at[a, 1 + 4 * c + pair[a]]
                else:
                    src, dst = v2.at[c, a, slots[n]], rz2.at[a, 4 * c + pair[a]]
                out.append(move(f, c, ST_Z + 3 * a + n, src, dst, devs[n]))
        return out

    def go(copies):
        for d in copies:
            d.start()

    def arrived(copies):
        for d in copies:
            d.wait_recv()

    def stage_1(f, c):
        arrived(d_q(f, c))
        for a in range(2):
            own = g[f, a, pl.ds(PER_CHUNK * c + 2 * pair[a], 2)].reshape(96, 128)
            x = jnp.concatenate([own] + [rq[f, c, a, n].reshape(96, 128) for n in range(3)], axis=1)
            s[f, c, a] = dot3(x, tab[0, a, 0:512], tab[1, a, 0:512], ((1,), (0,))).reshape(2, 3, 16, 256)
            go(d_2(f, c, (a,)))

    def stage_2(f, c):
        arrived(d_2(f, c))
        for a in range(2):
            u[f, c, a] = s[f, c, a, second_bit[a]] + r2[f, c, a]
        go(d_c(f, c))

    def stage_3(f, c):
        arrived(d_c(f, c))
        for a in range(2):
            t[f, c, a, second_bit[a]] = (u[f, c, a] + ru[f, c, a]) * wts[16 * a : 16 * a + 16][None]
        go(d_3(f, c))

    def stage_4(f, c):
        arrived(d_3(f, c))
        for a in range(2):
            x = t[f, c, a].reshape(96, 256)
            if f == 0:
                y = dot3(x, tab[0, a], tab[1, a], ((1,), (1,))).reshape(6, 16, 640)
                border_lanes = lane % 32
                before = y[0, :, 512:640]
                for n, source in ((1, 2), (2, 3), (3, 5)):
                    before = jnp.where(border_lanes == n, y[source, :, 512:640], before)
                for n in range(3):
                    v1[c, a, n, 0:6] = y[:, :, 128 * n + 128 : 128 * n + 256]
                    v1[c, a, n, 6] = before
                go(d_z(f, c, (a,)))
                rz1[a, 1 + 4 * c + pair[a], 0:6] = y[:, :, 0:128]
                rz1[a, 1 + 4 * c + pair[a], 6] = before
            else:
                y = dot3(x, tab[0, a, 0:512], tab[1, a, 0:512], ((1,), (1,))).reshape(6, 16, 512)
                for n in range(3):
                    v2[c, a, n] = y[:, :, 128 * n + 128 : 128 * n + 256]
                go(d_z(f, c, (a,)))
                rz2[a, 4 * c + pair[a]] = y[:, :, 0:128]

    def put(f, k, n, x):
        g[f, 0, k, n] = x[0:16]
        g[f, 1, k, n] = x[16:32]

    def begin_h(c):
        def body(k, _):
            for n, x in enumerate(magnetic(k, 0, NF)):
                put(0, k, n, x)
            return 0

        lax.fori_loop(PER_CHUNK * c, PER_CHUNK * c + PER_CHUNK, body, 0)
        go(d_q(0, c))

    below = jnp.where(gz == 0, 0.0, 1.0)

    def electric_inner(k, _):
        at, l = 1 + k // 2, k % 2
        prev_at, prev_l = (k + 1) // 2, (k + 1) % 2
        owner = at - 1 - 4 * (k // 8)

        def get(place, which, n):
            return jnp.concatenate([rz1[0, place, 3 * which + n], rz1[1, place, 3 * which + n]], axis=0)

        hr, hp, hz = (get(at, l, n) for n in range(3))
        hr_below, hp_below = get(prev_at, prev_l, 0), get(prev_at, prev_l, 1)
        own_q, own_b = owner // 2, owner % 2
        off_q = own_q + q - 2 * own_q * q
        marks = []
        for a in range(2):
            off_b = own_b + first_bit[a] - 2 * own_b * first_bit[a]
            marks.append(32 * (off_q + 2 * off_b) + 2 * l)

        def behind(x, n):
            edge = jnp.concatenate(
                [pltpu.roll(rz1[a, at, 6], (128 - marks[a] - n) % 128, 1) for a in range(2)], axis=0
            )
            return x - jnp.where(lane == 0, edge, pltpu.roll(x, 1, 1))

        keep, drive = ki[k, 0], ki[k, 1]
        back = pltpu.roll(hp, 1, 0)
        put(1, k, 0, keep * er[k, 0:NF] + drive * (coef[C_RC, 0:NF] * behind(hz, 1) - (hp - hp_below)))
        put(
            1, k, 1,
            keep * ea[k, 0:NF] + drive * ((hr - hr_below) - (hp - coef[C_KEEP_PREV, 0:NF] * back)),
        )
        put(
            1, k, 2,
            keep * eh[k, 0:NF]
            + drive * (coef[C_P, 0:NF] * hp - coef[C_Q, 0:NF] * back - coef[C_RN, 0:NF] * behind(hr, 0)),
        )
        return 0

    def begin_e(c):
        lax.fori_loop(PER_CHUNK * c, PER_CHUNK * c + PER_CHUNK, electric_inner, 0)
        go(d_q(1, c))

    def inner_factors(k, _):
        keep, drive = factors(k, 0, NF)
        ki[k, 0] = keep
        ki[k, 1] = drive
        return 0

    def tables():
        for number in range(NMAT):
            eps = jnp.full((8, 128), perm[number], F32)
            sig = jnp.full((8, 128), cond[number], F32)
            loss = sig * dt / (2.0 * eps)
            ktab[0, number] = (1.0 - loss) / (1.0 + loss)
            ktab[1, number] = dt / (eps * (1.0 + loss))
        mode = lax.broadcasted_iota(jnp.int32, (NF, 128), 1)
        wrow = lax.broadcasted_iota(jnp.int32, (NF, 128), 0)
        cuts = jnp.zeros((NF, 128), jnp.int32)
        for number in range(NF):
            cuts = jnp.where(wrow == number, cut[number], cuts)
        weight = jnp.where(mode == 0, 1.0 / NPHI, 2.0 / NPHI)
        weight = jnp.where(mode <= cuts, weight, 0.0)
        wts[:, 0:128] = weight
        wts[:, 128:256] = weight

    def outer_h(k, _):
        hr, hp, hz = magnetic(k, NF, NR)
        ho[k + 1, 0, 8:104] = hr
        ho[k + 1, 1, 8:104] = hp
        o_hz[k] = hz
        p2s[...] = jnp.where(
            lane == k,
            pltpu.roll(hr, k + 1, 1),
            jnp.where(lane == HALO_R + k, pltpu.roll(hz, HALO_R + k + 1, 1), p2s[...]),
        )
        return 0

    def last_inner_row(k, _):
        ho[k + 1, 1, 0:8] = rz1[1, 1 + k // 2, 3 * (k % 2) + 1, 8:16]
        return 0

    def outer_e(k, _):
        hr, hp, hz = ho[k + 1, 0, 8:104], ho[k + 1, 1, 8:104], o_hz[k]
        back = ho[k + 1, 1, 7:103]
        keep, drive = factors(k, NF, NR)

        def behind(x, n):
            return x - jnp.where(lane == 0, pltpu.roll(p2r[...], (128 - n) % 128, 1), pltpu.roll(x, 1, 1))

        o_er[k] = keep * er[k, NF:NR] + drive * (coef[C_RC, NF:NR] * behind(hz, HALO_R + k) - (hp - ho[k, 1, 8:104]))
        o_ea[k] = keep * ea[k, NF:NR] + drive * ((hr - ho[k, 0, 8:104]) - (hp - back))
        o_eh[k] = keep * eh[k, NF:NR] + drive * (
            coef[C_P, NF:NR] * hp - coef[C_Q, NF:NR] * back - coef[C_RN, NF:NR] * behind(hr, k)
        )
        return 0

    def run(body, lo, hi):
        lax.fori_loop(lo, hi, body, 0)

    begin_h(0)
    begin_h(1)
    begin_h(2)
    tables()
    loads[6][0].wait()
    stage_1(0, 0)
    for n in range(7):
        loads[n][1].wait()
    pack_first(NF, NR)
    b_p1o.start()
    stage_1(0, 1)
    run(inner_factors, 0, 12)
    stage_2(0, 0)
    stage_1(0, 2)
    run(inner_factors, 12, 24)
    stage_2(0, 1)
    b_p1o.wait_recv()
    run(outer_h, 18, 24)
    stage_3(0, 0)
    stage_2(0, 2)
    b_ho.start()
    run(outer_h, 12, 18)
    stage_3(0, 1)
    stage_4(0, 0)
    run(outer_h, 6, 12)
    stage_3(0, 2)
    stage_4(0, 1)
    run(outer_h, 0, 6)
    b_p2.start()
    arrived(d_z(0, 0))
    stage_4(0, 2)
    arrived(d_z(0, 1))
    begin_e(1)
    arrived(d_z(0, 2))
    b_hi.start()
    b_hi2.start()
    begin_e(2)
    b_hi.wait_recv()
    b_hi2.wait_recv()
    for a in range(2):
        rz1[a, 0, 3:5] = rz1[a, 0, 3:5] * below
    begin_e(0)
    stage_1(1, 1)
    run(last_inner_row, 0, LAYERS)
    b_p2.wait_recv()
    b_ho.wait_recv()
    ho[0, :, 8:104] = ho[0, :, 8:104] * below
    stage_1(1, 2)
    run(outer_e, 0, 4)
    stage_2(1, 1)
    stage_1(1, 0)
    run(outer_e, 4, 8)
    stage_2(1, 2)
    run(outer_e, 8, 12)
    stage_3(1, 1)
    stage_2(1, 0)
    run(outer_e, 12, 16)
    stage_3(1, 2)
    stage_4(1, 1)
    run(outer_e, 16, 20)
    stage_3(1, 0)
    stage_4(1, 2)
    run(outer_e, 20, 24)
    stage_4(1, 0)
    for c in (1, 2, 0):
        arrived(d_z(1, c))

    for f in range(2):
        for c in range(CHUNKS):
            for kind in (d_q, d_2, d_c, d_3, d_z):
                for d in kind(f, c):
                    d.wait_send()
    for d in (b_er, b_ea, b_p1i, b_p1o, b_p2, b_hi, b_hi2, b_ho):
        d.wait_send()


def local(er, ea, eh, mr, mp, mz, material, permittivity, conductivity, mode_cutoff):
    base, phase = basis_tables()
    anywhere = pl.BlockSpec(memory_space=pltpu.HBM)
    vmem = pl.BlockSpec(memory_space=pltpu.VMEM)

    def scratch(*shape, dtype=F32):
        return pltpu.VMEM(shape, dtype)

    field = (LAYERS, NR, WIDTH)
    outer = (LAYERS, OUT, WIDTH)
    held = (
        scratch(LAYERS + 1, 2, OUT + 8, WIDTH),
        scratch(*outer),
        scratch(*outer),
        scratch(*outer),
        scratch(*outer),
        scratch(2, PAIRS + 1, 7, 16, WIDTH),
        scratch(2, PAIRS, 6, 16, WIDTH),
    )
    step = pl.pallas_call(
        kernel,
        out_shape=held,
        in_specs=[anywhere] * 12,
        out_specs=tuple([vmem] * 7),
        scratch_shapes=[
            scratch(LAYERS + 1, NR, WIDTH),
            scratch(LAYERS + 1, NR + 8, WIDTH),
            scratch(LAYERS, NR + 8, WIDTH),
            scratch(*field),
            scratch(*field),
            scratch(*field),
            scratch(*field, dtype=jnp.int32),
            pltpu.SMEM((NMAT,), F32),
            pltpu.SMEM((NMAT,), F32),
            pltpu.SMEM((NF,), jnp.int32),
            scratch(*base.shape),
            scratch(*phase.shape),
            scratch(9, NR, 128),
            scratch(2, NMAT, 8, 128),
            scratch(NF, 256),
            scratch(2, 2, 640, 256, dtype=BF16),
            scratch(NR, 128),
            scratch(NR, 128),
            scratch(OUT, 128),
            scratch(OUT, 128),
            scratch(2, 2, LAYERS, 3, 16, 128),
            scratch(2, CHUNKS, 2, 3, 2, 3, 16, 128),
            scratch(2, CHUNKS, 2, 2, 3, 16, 256),
            scratch(2, CHUNKS, 2, 3, 16, 256),
            scratch(2, CHUNKS, 2, 3, 16, 256),
            scratch(2, CHUNKS, 2, 3, 16, 256),
            scratch(2, CHUNKS, 2, 2, 3, 16, 256),
            scratch(CHUNKS, 2, 3, 7, 16, 128),
            scratch(CHUNKS, 2, 3, 6, 16, 128),
            scratch(LAYERS, 2, NF, 128),
            pltpu.SemaphoreType.DMA((19,)),
            pltpu.SemaphoreType.DMA((2 * CHUNKS, NSTAGE)),
            pltpu.SemaphoreType.DMA((2 * CHUNKS, NSTAGE)),
            pltpu.SemaphoreType.DMA((8,)),
            pltpu.SemaphoreType.DMA((8,)),
        ],
        compiler_params=pltpu.CompilerParams(
            collective_id=0, has_side_effects=True, vmem_limit_bytes=40 * 1024 * 1024
        ),
        name="yee_step",
    )
    operands = (
        er, ea, eh, mr, mp, mz, material, permittivity, conductivity, mode_cutoff,
        jnp.asarray(base), jnp.asarray(phase),
    )
    return rows_out(*step(*(pltpu.with_memory_space_constraint(x, pltpu.HBM) for x in operands)))


def rows_out(ho, o_hz, o_er, o_ea, o_eh, rz1, rz2):
    vmem = pl.BlockSpec(memory_space=pltpu.VMEM)
    hbm = pl.BlockSpec(memory_space=pltpu.HBM)
    return pl.pallas_call(
        write_kernel,
        out_shape=tuple(jax.ShapeDtypeStruct((LAYERS, NR, WIDTH), F32) for _ in range(6)),
        in_specs=[vmem] * 7,
        out_specs=tuple([hbm] * 6),
        scratch_shapes=[pltpu.SemaphoreType.DMA((40,))],
        compiler_params=pltpu.CompilerParams(vmem_limit_bytes=1024 * 1024),
        name="write_fields",
    )(ho, o_hz, o_er, o_ea, o_eh, rz1, rz2)

def write_kernel(ho, o_hz, o_er, o_ea, o_eh, rz1, rz2, w_er, w_ea, w_eh, w_hr, w_hp, w_hz, sem):
    copies = []

    def add(src, dst):
        copies.append(pltpu.make_async_copy(src, dst, sem.at[len(copies)]))

    for o, w in ((o_hz, w_hz), (o_er, w_er), (o_ea, w_ea), (o_eh, w_eh)):
        add(o, w.at[:, NF:NR])
    for n, w in ((0, w_hr), (1, w_hp)):
        add(ho.at[1 : LAYERS + 1, n, 8:104], w.at[:, NF:NR])
    for l in range(2):
        for a in range(2):
            rows = slice(16 * a, 16 * a + 16)
            for n, w in enumerate((w_hr, w_hp, w_hz)):
                add(rz1.at[a, 1 : PAIRS + 1, 3 * l + n], w.reshape(PAIRS, 2, NR, WIDTH).at[:, l, rows])
            for n, w in enumerate((w_er, w_ea, w_eh)):
                add(rz2.at[a, :, 3 * l + n], w.reshape(PAIRS, 2, NR, WIDTH).at[:, l, rows])
    for d in copies:
        d.start()
    for d in copies:
        d.wait()


def solution(mesh):
    field = P("gz", None, "phi")
    return jax.shard_map(
        local,
        mesh=mesh,
        in_specs=(field,) * 7 + (P(),) * 3,
        out_specs=(field,) * 6,
        check_vma=False,
    )
```

time: 98.5 us -> 84.6 us (0.86)
  local copies, waits for them, and re-layouts: 10.5 us -> 0 us
  Pallas kernels: 87.1 us -> 83.8 us
    unnamed x16 -> x0, local copies, waits for them, and re-layouts: 10.5 us -> none
    pallas_call x1 -> x2, Pallas kernels: 87.1 us -> 83.8 us  [the longest x1 79.9 us: local(): step(*(pltpu.with_memory_space_constraint(x, pltpu.HBM) for x in operands))]
where the time goes in v2:
time: 84.6 us; the launch traced here: 84.5 us
  Pallas kernels  83.8 us (99%)
    pallas_call x1, Pallas kernels, local(): step(*(pltpu.with_memory_space_constraint(x, pltpu.HBM) for x in operands))  79.9 us
    pallas_call x1, Pallas kernels, rows_out(): pl.pallas_call(write_kernel, out_shape=tuple((jax.ShapeDtypeStruct((LAYER...  3.94 us

profile of v2, /device:TPU:1, one launch (start us, length us, event | category | flops | bytes accessed | tf_op | source)
XLA Modules:
  0.0 84.5 jit_solution(6885312674694483684)
XLA Ops:
  0.6 79.9 %yee_step.1 = (f32[25,2,104,128]{3,2,1,0:T(8,128)S(1)}, f32[24,96,128]{2,1,0:T(8,128)S(1)}, f32[24,96,128]{2,1,0:T(8,128)S(1)}, f32[24,96,128]{2,1,0:T(8,128)S(1...) custom-call(f32[24,128,128]{2,1,0:T(8,128)} %er_h.1, ...), custom_call_target="tpu_custom_call" | custom-call | tf_op jit(solution)/shard_map/yee_step/pallas_call | solution.py:600
  80.5 3.9 %write_fields.1 = (f32[24,128,128]{2,1,0:T(8,128)}, f32[24,128,128]{2,1,0:T(8,128)}, f32[24,128,128]{2,1,0:T(8,128)}, f32[24,128,128]{2,1,0:T(8,128)}, f32[24,128,128]{2,1,0:T(8,128)}, /*index=5*/f32[24,128,128]{2,1,0:T(8,128)}) custom-call(f32[25,2,104,128]{3,2,1,0:T(8,128)S(1)} %get-tuple-element.13.ho, f32[24,96,128]{2,1,0:T(8,128)S(1)} %get-tuple-element.14.o_hz, ...), custom_call_target="tpu_custom_call" | custom-call | tf_op jit(solution)/shard_map/write_fields/pallas_call | solution.py:606

commit v3 on v2

--- a/solution.py
+++ b/solution.py
@@ -17,8 +17,8 @@
 LAYERS = 24
 WIDTH = 128
 CHUNKS = 3
-PER_CHUNK = 8
-PAIRS = LAYERS // 2
+PER_CHUNK = LAYERS // CHUNKS
+HELD = PER_CHUNK // 4
 HALO_R = 32
 
 inner_radius = 64.0
@@ -31,7 +31,8 @@
 C_DT_RN, C_UP, C_HERE, C_DT_RC, C_RC, C_KEEP_PREV, C_P, C_Q, C_RN = range(9)
 ST_Q, ST_2, ST_C, ST_3, ST_Z = 0, 6, 8, 9, 11
 NSTAGE = 17
-B_P1I, B_P1O, B_ER, B_EA, B_P2, B_HI, B_HI2, B_HO = range(8)
+B_P1O, B_ER, B_EA, B_P2, B_HO, B_P1Q, B_HI = 0, 1, 2, 3, 4, 5, 10
+NBORDER = 20
 
 
 def basis_tables():
@@ -57,7 +58,9 @@
     def dot(a, b):
         return lax.dot_general(a, b, (dims, ((), ())), preferred_element_type=F32)
 
-    return dot(hi, b_hi) + dot(lo, b_hi) + dot(hi, b_lo)
+    m = x.shape[0]
+    high = dot(jnp.concatenate([hi, lo], axis=0), b_hi)
+    return high[0:m] + high[m : 2 * m] + dot(hi, b_lo)
 
 
 def kernel(
@@ -66,7 +69,7 @@
     er, ea, eh, mr, mp, mz, mat,
     perm, cond, cut, base, phase,
     coef, ktab, wts, tab,
-    p1s, p1r, p2s, p2r,
+    p1s, p1r, p1q, p2s, p2r,
     g, rq, s, r2, u, ru, t, v1, v2, ki,
     in_sem, send, recv, bsend, brecv,
 ):
@@ -112,10 +115,12 @@
         loads.append((inner, outer))
 
     barrier = pltpu.get_barrier_semaphore()
-    for d in (sib, dev_z1, sib_z1, dev_z3, sib_z3, dev_y, nxt, prv):
+    quads = (sib, dev_z1, sib_z1, dev_z3, sib_z3)
+    for d in quads + (dev_y, nxt, prv):
         pl.semaphore_signal(barrier, inc=1, device_id={"phi": d}, device_id_type=MESH)
-    for d in (up, down):
-        pl.semaphore_signal(barrier, inc=1, device_id={"gz": d}, device_id_type=MESH)
+    for slab in (up, down):
+        for d in quads + (phi,):
+            pl.semaphore_signal(barrier, inc=1, device_id={"phi": d, "gz": slab}, device_id_type=MESH)
     for inner, _ in loads[0:2]:
         inner.start()
     for d in small:
@@ -136,31 +141,6 @@
             return 0
 
         lax.fori_loop(0, LAYERS, body, 0)
-
-    loads[0][0].wait()
-    loads[1][0].wait()
-    pack_first(0, NF)
-
-    pl.semaphore_wait(barrier, 10)
-
-    def border(src, dst, n, dev):
-        return pltpu.make_async_remote_copy(
-            src_ref=src, dst_ref=dst, send_sem=bsend.at[n], recv_sem=brecv.at[n],
-            device_id=dev, device_id_type=MESH,
-        )
-
-    b_er = border(er_h.at[0], er.at[LAYERS], B_ER, {"gz": down})
-    b_ea = border(ea_h.at[0], ea.at[LAYERS, 0:NR], B_EA, {"gz": down})
-    b_p1i = border(p1s.at[0:NF], p1r.at[0:NF], B_P1I, {"phi": prv})
-    b_p1o = border(p1s.at[NF:NR], p1r.at[NF:NR], B_P1O, {"phi": prv})
-    b_p2 = border(p2s, p2r, B_P2, {"phi": nxt})
-    b_hi = border(rz1.at[0, PAIRS, 3:5], rz1.at[0, 0, 3:5], B_HI, {"gz": up})
-    b_hi2 = border(rz1.at[1, PAIRS, 3:5], rz1.at[1, 0, 3:5], B_HI2, {"gz": up})
-    b_ho = border(ho.at[LAYERS, :, 8:104], ho.at[0, :, 8:104], B_HO, {"gz": up})
-
-    b_p1i.start()
-    b_er.start()
-    b_ea.start()
 
     def clear(k, _):
         eh[k, NR : NR + 8] = jnp.zeros((8, 128), F32)
@@ -183,39 +163,23 @@
     coef[C_P] = rc * inv_rn
     coef[C_Q] = jnp.where(first, 0.0, (rc - 1.0) * inv_rn)
     coef[C_RN] = (1.0 / dphi) * inv_rn
-    for d in small:
-        d.wait()
-
-    for kind in range(2):
-        for place, who in enumerate((phi, sib) + first_dev[kind]):
-            pc = phase[0, pl.ds(who, 1), :]
-            ps = phase[1, pl.ds(who, 1), :]
-            if kind == 1 and place < 2:
-                tab[:, 1, place * 128 : place * 128 + 128] = tab[:, 0, place * 128 : place * 128 + 128]
-            else:
-                for part, m in ((0, base[0, 0:128] * pc - base[1, 0:128] * ps), (1, base[1, 0:128] * pc + base[0, 0:128] * ps)):
-                    h, l = split(m)
-                    tab[0, kind, place * 128 : place * 128 + 128, part * 128 : part * 128 + 128] = h
-                    tab[1, kind, place * 128 : place * 128 + 128, part * 128 : part * 128 + 128] = l
-            bc, bs = base[0, 128:129], base[1, 128:129]
-            lo_row = 512 + place * 32
-            for part, m in ((0, bc * pc - bs * ps), (1, bs * pc + bc * ps)):
-                h, l = split(jnp.broadcast_to(m, (32, 128)))
-                tab[0, kind, lo_row : lo_row + 32, part * 128 : part * 128 + 128] = h
-                tab[1, kind, lo_row : lo_row + 32, part * 128 : part * 128 + 128] = l
-
-    for n in range(2, 6):
-        loads[n][0].wait()
-    b_er.wait_recv()
-    b_ea.wait_recv()
-    above = jnp.where(gz == 7, 0.0, 1.0)
-    er[LAYERS] = er[LAYERS] * above
-    ea[LAYERS, 0:NR] = ea[LAYERS, 0:NR] * above
-    b_p1i.wait_recv()
+    def border(src, dst, n, dev, arrival=None):
+        return pltpu.make_async_remote_copy(
+            src_ref=src, dst_ref=dst, send_sem=bsend.at[n], recv_sem=brecv.at[n if arrival is None else arrival],
+            device_id=dev, device_id_type=MESH,
+        )
+
+    b_er = border(er_h.at[0], er.at[LAYERS], B_ER, {"gz": down})
+    b_ea = border(ea_h.at[0], ea.at[LAYERS, 0:NR], B_EA, {"gz": down})
+    b_p1q = [border(p1s.at[0:NF], p1q.at[n], B_P1Q + n, {"phi": d}) for n, d in enumerate(quads)]
+    b_p1o = border(p1s.at[NF:NR], p1r, B_P1O, {"phi": prv})
+    b_p2 = border(p2s, p2r, B_P2, {"phi": nxt})
+    b_ho = border(ho.at[LAYERS, :, 8:104], ho.at[0, :, 8:104], B_HO, {"gz": up})
 
     def magnetic(k, lo, hi):
         def ahead(x, n):
-            return jnp.where(lane == 127, pltpu.roll(p1r[lo:hi], 127 - n, 1), pltpu.roll(x, 127, 1)) - x
+            edge = 0.0 if lo == 0 else pltpu.roll(p1r[...], 127 - n, 1)
+            return jnp.where(lane == 127, edge, pltpu.roll(x, 127, 1)) - x
 
         e_h = eh[k, lo:hi]
         e_r = er[k, lo:hi]
@@ -250,17 +214,20 @@
         out = []
         for a in range(2):
             b = first_bit[a]
-            pairs = (2 * q + 1 - b, 2 * (1 - q) + 1 - b, 2 * (1 - q) + b)
+            owners = (2 * q + 1 - b, 2 * (1 - q) + 1 - b, 2 * (1 - q) + b)
             devs = first_dev[a] + (sib,)
             slots = (1, 2, 0)
             for n in range(3):
-                src = g.at[f, a, pl.ds(PER_CHUNK * c + 2 * pairs[n], 2)]
+                src = g.at[f, a, pl.ds(PER_CHUNK * c + HELD * owners[n], HELD)]
                 out.append(move(f, c, ST_Q + 3 * a + n, src, rq.at[f, c, a, slots[n]], devs[n]))
         return out
 
+    def eight(bit):
+        return pl.ds(pl.multiple_of(8 * bit, 8), 8)
+
     def d_2(f, c, sets=(0, 1)):
         return [
-            move(f, c, ST_2 + a, s.at[f, c, a, 1 - second_bit[a]], r2.at[f, c, a], second_dev[a])
+            move(f, c, ST_2 + a, s.at[f, c, a, :, :, eight(1 - second_bit[a])], r2.at[f, c, a], second_dev[a])
             for a in sets
         ]
 
@@ -270,7 +237,7 @@
     def d_3(f, c):
         out = []
         for a in range(2):
-            own = t.at[f, c, a, second_bit[a]]
+            own = t.at[f, c, a, :, :, eight(second_bit[a])]
             out.append(move(f, c, ST_3 + a, own, own, second_dev[a]))
         return out
 
@@ -281,15 +248,26 @@
             slots = (1, 2, 0)
             for n in range(3):
                 if f == 0:
-                    src, dst = v1.at[c, a, slots[n]], rz1.at[a, 1 + 4 * c + pair[a]]
+                    src, dst = v1.at[c, a, slots[n]], rz1.at[a, pl.ds(1 + PER_CHUNK * c + HELD * pair[a], HELD)]
                 else:
-                    src, dst = v2.at[c, a, slots[n]], rz2.at[a, 4 * c + pair[a]]
+                    src, dst = v2.at[c, a, slots[n]], rz2.at[a, pl.ds(PER_CHUNK * c + HELD * pair[a], HELD)]
                 out.append(move(f, c, ST_Z + 3 * a + n, src, dst, devs[n]))
         return out
+
+    def d_up(a):
+        devs = (sib,) + first_dev[a] + (phi,)
+        srcs = [v1.at[CHUNKS - 1, a, n, HELD - 1, 0:2] for n in range(3)] + [rz1.at[a, LAYERS, 0:2]]
+        return [
+            border(srcs[n], rz1.at[a, 0, 0:2], B_HI + 4 * a + n, {"phi": devs[n], "gz": up}, B_HI + a)
+            for n in range(4)
+        ]
+
+    started = []
 
     def go(copies):
         for d in copies:
             d.start()
+            started.append(d)
 
     def arrived(copies):
         for d in copies:
@@ -298,81 +276,104 @@
     def stage_1(f, c):
         arrived(d_q(f, c))
         for a in range(2):
-            own = g[f, a, pl.ds(PER_CHUNK * c + 2 * pair[a], 2)].reshape(96, 128)
-            x = jnp.concatenate([own] + [rq[f, c, a, n].reshape(96, 128) for n in range(3)], axis=1)
-            s[f, c, a] = dot3(x, tab[0, a, 0:512], tab[1, a, 0:512], ((1,), (0,))).reshape(2, 3, 16, 256)
+            k = PER_CHUNK * c + HELD * pair[a]
+            own = g[f, a, pl.ds(k, HELD)].reshape(48 * HELD, 128)
+            parts = [own] + [rq[f, c, a, n].reshape(48 * HELD, 128) for n in range(3)]
+            width = 512
+            if f == 0:
+                rows = slice(16 * a, 16 * a + 16)
+                tiles = [p1s[rows]] + [p1q[n, rows] for n in ((0, 1, 2), (0, 3, 4))[a]]
+                extra = []
+                for l in range(HELD):
+                    height = jnp.zeros((16, 128), F32)
+                    radial = jnp.zeros((16, 128), F32)
+                    for m in range(4):
+                        here = lane == 32 * m
+                        height = jnp.where(here, pltpu.roll(tiles[m], (32 * m + 128 - k - l) % 128, 1), height)
+                        radial = jnp.where(here, pltpu.roll(tiles[m], (32 * m + 128 - HALO_R - k - l) % 128, 1), radial)
+                    extra += [-coef[C_DT_RN, rows] * height, jnp.zeros((16, 128), F32), coef[C_DT_RC, rows] * radial]
+                parts.append(jnp.concatenate(extra, axis=0))
+                width = 640
+            x = jnp.concatenate(parts, axis=1)
+            s[f, c, a] = dot3(x, tab[0, a, 0:width], tab[1, a, 0:width], ((1,), (0,))).reshape(HELD, 3, 16, 256)
             go(d_2(f, c, (a,)))
 
     def stage_2(f, c):
         arrived(d_2(f, c))
         for a in range(2):
-            u[f, c, a] = s[f, c, a, second_bit[a]] + r2[f, c, a]
+            u[f, c, a] = s[f, c, a, :, :, eight(second_bit[a])] + r2[f, c, a]
         go(d_c(f, c))
 
     def stage_3(f, c):
         arrived(d_c(f, c))
         for a in range(2):
-            t[f, c, a, second_bit[a]] = (u[f, c, a] + ru[f, c, a]) * wts[16 * a : 16 * a + 16][None]
+            w = wts[pl.ds(pl.multiple_of(16 * a + 8 * second_bit[a], 8), 8)]
+            t[f, c, a, :, :, eight(second_bit[a])] = (u[f, c, a] + ru[f, c, a]) * w[None, None]
         go(d_3(f, c))
 
     def stage_4(f, c):
         arrived(d_3(f, c))
         for a in range(2):
-            x = t[f, c, a].reshape(96, 256)
+            x = t[f, c, a].reshape(48 * HELD, 256)
+            k = PER_CHUNK * c + HELD * pair[a]
             if f == 0:
-                y = dot3(x, tab[0, a], tab[1, a], ((1,), (1,))).reshape(6, 16, 640)
-                border_lanes = lane % 32
-                before = y[0, :, 512:640]
-                for n, source in ((1, 2), (2, 3), (3, 5)):
-                    before = jnp.where(border_lanes == n, y[source, :, 512:640], before)
+                y = dot3(x, tab[0, a], tab[1, a], ((1,), (1,))).reshape(HELD, 3, 16, 640)
+                before = jnp.where(lane % 32 == 0, y[:, 0, :, 512:640], y[:, 2, :, 512:640])
                 for n in range(3):
-                    v1[c, a, n, 0:6] = y[:, :, 128 * n + 128 : 128 * n + 256]
-                    v1[c, a, n, 6] = before
+                    v1[c, a, n, :, 0:3] = y[..., 128 * n + 128 : 128 * n + 256]
+                    v1[c, a, n, :, 3] = before
                 go(d_z(f, c, (a,)))
-                rz1[a, 1 + 4 * c + pair[a], 0:6] = y[:, :, 0:128]
-                rz1[a, 1 + 4 * c + pair[a], 6] = before
+                rz1[a, pl.ds(1 + k, HELD), 0:3] = y[..., 0:128]
+                rz1[a, pl.ds(1 + k, HELD), 3] = before
+                if c == CHUNKS - 1:
+
+                    @pl.when(pair[a] == 3)
+                    def _():
+                        for d in d_up(a):
+                            d.start()
+
             else:
-                y = dot3(x, tab[0, a, 0:512], tab[1, a, 0:512], ((1,), (1,))).reshape(6, 16, 512)
+                y = dot3(x, tab[0, a, 0:512], tab[1, a, 0:512], ((1,), (1,))).reshape(HELD, 3, 16, 512)
                 for n in range(3):
-                    v2[c, a, n] = y[:, :, 128 * n + 128 : 128 * n + 256]
+                    v2[c, a, n] = y[..., 128 * n + 128 : 128 * n + 256]
                 go(d_z(f, c, (a,)))
-                rz2[a, 4 * c + pair[a]] = y[:, :, 0:128]
+                rz2[a, pl.ds(k, HELD)] = y[..., 0:128]
+
+    def stage_5(f, c):
+        arrived(d_z(f, c))
 
     def put(f, k, n, x):
         g[f, 0, k, n] = x[0:16]
         g[f, 1, k, n] = x[16:32]
 
-    def begin_h(c):
+    def update_h(lo, hi):
         def body(k, _):
             for n, x in enumerate(magnetic(k, 0, NF)):
                 put(0, k, n, x)
             return 0
 
-        lax.fori_loop(PER_CHUNK * c, PER_CHUNK * c + PER_CHUNK, body, 0)
-        go(d_q(0, c))
+        lax.fori_loop(lo, hi, body, 0)
 
     below = jnp.where(gz == 0, 0.0, 1.0)
 
     def electric_inner(k, _):
-        at, l = 1 + k // 2, k % 2
-        prev_at, prev_l = (k + 1) // 2, (k + 1) % 2
-        owner = at - 1 - 4 * (k // 8)
-
-        def get(place, which, n):
-            return jnp.concatenate([rz1[0, place, 3 * which + n], rz1[1, place, 3 * which + n]], axis=0)
-
-        hr, hp, hz = (get(at, l, n) for n in range(3))
-        hr_below, hp_below = get(prev_at, prev_l, 0), get(prev_at, prev_l, 1)
+        owner = (k % PER_CHUNK) // HELD
+
+        def get(place, n):
+            return jnp.concatenate([rz1[0, place, n], rz1[1, place, n]], axis=0)
+
+        hr, hp, hz = (get(k + 1, n) for n in range(3))
+        hr_below, hp_below = get(k, 0), get(k, 1)
         own_q, own_b = owner // 2, owner % 2
         off_q = own_q + q - 2 * own_q * q
         marks = []
         for a in range(2):
             off_b = own_b + first_bit[a] - 2 * own_b * first_bit[a]
-            marks.append(32 * (off_q + 2 * off_b) + 2 * l)
+            marks.append(32 * (off_q + 2 * off_b))
 
         def behind(x, n):
             edge = jnp.concatenate(
-                [pltpu.roll(rz1[a, at, 6], (128 - marks[a] - n) % 128, 1) for a in range(2)], axis=0
+                [pltpu.roll(rz1[a, k + 1, 3], (128 - marks[a] - n) % 128, 1) for a in range(2)], axis=0
             )
             return x - jnp.where(lane == 0, edge, pltpu.roll(x, 1, 1))
 
@@ -399,6 +400,29 @@
         ki[k, 0] = keep
         ki[k, 1] = drive
         return 0
+
+    def basis():
+        for d in small:
+            d.wait()
+
+        for kind in range(2):
+            for place, who in enumerate((phi, sib) + first_dev[kind]):
+                pc = phase[0, pl.ds(who, 1), :]
+                ps = phase[1, pl.ds(who, 1), :]
+                if kind == 1 and place < 2:
+                    tab[:, 1, place * 128 : place * 128 + 128] = tab[:, 0, place * 128 : place * 128 + 128]
+                else:
+                    for part, m in ((0, base[0, 0:128] * pc - base[1, 0:128] * ps), (1, base[1, 0:128] * pc + base[0, 0:128] * ps)):
+                        h, l = split(m)
+                        tab[0, kind, place * 128 : place * 128 + 128, part * 128 : part * 128 + 128] = h
+                        tab[1, kind, place * 128 : place * 128 + 128, part * 128 : part * 128 + 128] = l
+                bc, bs = base[0, 128:129], base[1, 128:129]
+                lo_row = 512 + place * 32
+                for part, m in ((0, bc * pc - bs * ps), (1, bs * pc + bc * ps)):
+                    h, l = split(jnp.broadcast_to(m, (32, 128)))
+                    tab[0, kind, lo_row : lo_row + 32, part * 128 : part * 128 + 128] = h
+                    tab[1, kind, lo_row : lo_row + 32, part * 128 : part * 128 + 128] = l
+
 
     def tables():
         for number in range(NMAT):
@@ -430,7 +454,7 @@
         return 0
 
     def last_inner_row(k, _):
-        ho[k + 1, 1, 0:8] = rz1[1, 1 + k // 2, 3 * (k % 2) + 1, 8:16]
+        ho[k + 1, 1, 0:8] = rz1[1, k + 1, 1, 8:16]
         return 0
 
     def outer_e(k, _):
@@ -451,80 +475,129 @@
     def run(body, lo, hi):
         lax.fori_loop(lo, hi, body, 0)
 
-    begin_h(0)
-    begin_h(1)
-    begin_h(2)
+    def outer_loaded():
+        for n in range(7):
+            loads[n][1].wait()
+        pack_first(NF, NR)
+        go([b_p1o])
+
+    def layer_above():
+        arrived([b_er, b_ea])
+        above = jnp.where(gz == 7, 0.0, 1.0)
+        er[LAYERS] = er[LAYERS] * above
+        ea[LAYERS, 0:NR] = ea[LAYERS, 0:NR] * above
+
+    def begin_h(c):
+        update_h(PER_CHUNK * c, PER_CHUNK * c + PER_CHUNK)
+        go(d_q(0, c))
+
+    def layer_below():
+        for a in range(2):
+            arrived(d_up(a)[0:1])
+            rz1[a, 0, 0:2] = rz1[a, 0, 0:2] * below
+
+    def outer_borders():
+        arrived([b_p2, b_ho])
+        ho[0, :, 8:104] = ho[0, :, 8:104] * below
+
+    def drain():
+        while started:
+            started.pop().wait_send()
+
+    for n in range(6):
+        loads[n][0].wait()
+    pack_first(0, NF)
+    update_h(0, PER_CHUNK)
+    pl.semaphore_wait(barrier, 20)
+    go([b_er, b_ea] + d_q(0, 0) + b_p1q)
+    if CHUNKS > 2:
+        begin_h(1)
+    basis()
+    layer_above()
+    if CHUNKS == 2:
+        begin_h(1)
     tables()
     loads[6][0].wait()
-    stage_1(0, 0)
-    for n in range(7):
-        loads[n][1].wait()
-    pack_first(NF, NR)
-    b_p1o.start()
-    stage_1(0, 1)
-    run(inner_factors, 0, 12)
-    stage_2(0, 0)
-    stage_1(0, 2)
-    run(inner_factors, 12, 24)
-    stage_2(0, 1)
-    b_p1o.wait_recv()
-    run(outer_h, 18, 24)
-    stage_3(0, 0)
-    stage_2(0, 2)
-    b_ho.start()
-    run(outer_h, 12, 18)
-    stage_3(0, 1)
-    stage_4(0, 0)
-    run(outer_h, 6, 12)
-    stage_3(0, 2)
-    stage_4(0, 1)
-    run(outer_h, 0, 6)
-    b_p2.start()
-    arrived(d_z(0, 0))
-    stage_4(0, 2)
-    arrived(d_z(0, 1))
-    begin_e(1)
-    arrived(d_z(0, 2))
-    b_hi.start()
-    b_hi2.start()
-    begin_e(2)
-    b_hi.wait_recv()
-    b_hi2.wait_recv()
+    arrived(b_p1q)
+
+    order = [
+        (begin_h, 2),
+        (outer_loaded,),
+        (run, inner_factors, 0, 6),
+        (run, inner_factors, 6, 12),
+        (run, inner_factors, 12, 18),
+        (run, inner_factors, 18, 24),
+        (arrived, [b_p1o]),
+        (stage_1, 0, 0),
+        (run, outer_h, 21, 24),
+        (go, [b_ho]),
+        (run, outer_h, 18, 21),
+        (stage_1, 0, 1),
+        (run, outer_h, 15, 18),
+        (run, outer_h, 12, 15),
+        (stage_1, 0, 2),
+        (stage_2, 0, 0),
+        (run, outer_h, 9, 12),
+        (run, outer_h, 6, 9),
+        (run, outer_h, 3, 6),
+        (stage_2, 0, 1),
+        (run, outer_h, 0, 3),
+        (go, [b_p2]),
+        (stage_2, 0, 2),
+        (stage_3, 0, 0),
+        (stage_3, 0, 1),
+        (stage_3, 0, 2),
+        (stage_4, 0, 0),
+        (stage_4, 0, 1),
+        (stage_4, 0, 2),
+        (stage_5, 0, 1),
+        (stage_5, 0, 0),
+        (begin_e, 1),
+        (stage_5, 0, 2),
+        (layer_below,),
+        (begin_e, 0),
+        (begin_e, 2),
+        (run, last_inner_row, 0, LAYERS),
+        (outer_borders,),
+        (run, outer_e, 0, 2),
+        (run, outer_e, 2, 4),
+        (run, outer_e, 4, 6),
+        (stage_1, 1, 1),
+        (run, outer_e, 6, 8),
+        (run, outer_e, 8, 10),
+        (stage_1, 1, 0),
+        (run, outer_e, 10, 12),
+        (run, outer_e, 12, 14),
+        (stage_1, 1, 2),
+        (stage_2, 1, 1),
+        (run, outer_e, 14, 16),
+        (run, outer_e, 16, 18),
+        (stage_2, 1, 0),
+        (run, outer_e, 18, 20),
+        (run, outer_e, 20, 22),
+        (run, outer_e, 22, 24),
+        (stage_2, 1, 2),
+        (stage_3, 1, 1),
+        (stage_3, 1, 0),
+        (stage_3, 1, 2),
+        (stage_4, 1, 1),
+        (stage_4, 1, 0),
+        (stage_4, 1, 2),
+        (drain,),
+        (stage_5, 1, 1),
+        (stage_5, 1, 2),
+        (stage_5, 1, 0),
+    ]
+    for step, *what in order:
+        step(*what)
+
+    drain()
     for a in range(2):
-        rz1[a, 0, 3:5] = rz1[a, 0, 3:5] * below
-    begin_e(0)
-    stage_1(1, 1)
-    run(last_inner_row, 0, LAYERS)
-    b_p2.wait_recv()
-    b_ho.wait_recv()
-    ho[0, :, 8:104] = ho[0, :, 8:104] * below
-    stage_1(1, 2)
-    run(outer_e, 0, 4)
-    stage_2(1, 1)
-    stage_1(1, 0)
-    run(outer_e, 4, 8)
-    stage_2(1, 2)
-    run(outer_e, 8, 12)
-    stage_3(1, 1)
-    stage_2(1, 0)
-    run(outer_e, 12, 16)
-    stage_3(1, 2)
-    stage_4(1, 1)
-    run(outer_e, 16, 20)
-    stage_3(1, 0)
-    stage_4(1, 2)
-    run(outer_e, 20, 24)
-    stage_4(1, 0)
-    for c in (1, 2, 0):
-        arrived(d_z(1, c))
-
-    for f in range(2):
-        for c in range(CHUNKS):
-            for kind in (d_q, d_2, d_c, d_3, d_z):
-                for d in kind(f, c):
-                    d.wait_send()
-    for d in (b_er, b_ea, b_p1i, b_p1o, b_p2, b_hi, b_hi2, b_ho):
-        d.wait_send()
+
+        @pl.when(pair[a] == 3)
+        def _():
+            for d in d_up(a):
+                d.wait_send()
 
 
 def local(er, ea, eh, mr, mp, mz, material, permittivity, conductivity, mode_cutoff):
@@ -543,8 +616,8 @@
         scratch(*outer),
         scratch(*outer),
         scratch(*outer),
-        scratch(2, PAIRS + 1, 7, 16, WIDTH),
-        scratch(2, PAIRS, 6, 16, WIDTH),
+        scratch(2, LAYERS + 1, 4, 16, WIDTH),
+        scratch(2, LAYERS, 3, 16, WIDTH),
     )
     step = pl.pallas_call(
         kernel,
@@ -569,24 +642,25 @@
             scratch(NF, 256),
             scratch(2, 2, 640, 256, dtype=BF16),
             scratch(NR, 128),
-            scratch(NR, 128),
+            scratch(OUT, 128),
+            scratch(5, NF, 128),
             scratch(OUT, 128),
             scratch(OUT, 128),
             scratch(2, 2, LAYERS, 3, 16, 128),
-            scratch(2, CHUNKS, 2, 3, 2, 3, 16, 128),
-            scratch(2, CHUNKS, 2, 2, 3, 16, 256),
-            scratch(2, CHUNKS, 2, 3, 16, 256),
-            scratch(2, CHUNKS, 2, 3, 16, 256),
-            scratch(2, CHUNKS, 2, 3, 16, 256),
-            scratch(2, CHUNKS, 2, 2, 3, 16, 256),
-            scratch(CHUNKS, 2, 3, 7, 16, 128),
-            scratch(CHUNKS, 2, 3, 6, 16, 128),
+            scratch(2, CHUNKS, 2, 3, HELD, 3, 16, 128),
+            scratch(2, CHUNKS, 2, HELD, 3, 16, 256),
+            scratch(2, CHUNKS, 2, HELD, 3, 8, 256),
+            scratch(2, CHUNKS, 2, HELD, 3, 8, 256),
+            scratch(2, CHUNKS, 2, HELD, 3, 8, 256),
+            scratch(2, CHUNKS, 2, HELD, 3, 16, 256),
+            scratch(CHUNKS, 2, 3, HELD, 4, 16, 128),
+            scratch(CHUNKS, 2, 3, HELD, 3, 16, 128),
             scratch(LAYERS, 2, NF, 128),
             pltpu.SemaphoreType.DMA((19,)),
             pltpu.SemaphoreType.DMA((2 * CHUNKS, NSTAGE)),
             pltpu.SemaphoreType.DMA((2 * CHUNKS, NSTAGE)),
-            pltpu.SemaphoreType.DMA((8,)),
-            pltpu.SemaphoreType.DMA((8,)),
+            pltpu.SemaphoreType.DMA((NBORDER,)),
+            pltpu.SemaphoreType.DMA((NBORDER,)),
         ],
         compiler_params=pltpu.CompilerParams(
             collective_id=0, has_side_effects=True, vmem_limit_bytes=40 * 1024 * 1024
@@ -623,13 +697,12 @@
         add(o, w.at[:, NF:NR])
     for n, w in ((0, w_hr), (1, w_hp)):
         add(ho.at[1 : LAYERS + 1, n, 8:104], w.at[:, NF:NR])
-    for l in range(2):
-        for a in range(2):
-            rows = slice(16 * a, 16 * a + 16)
-            for n, w in enumerate((w_hr, w_hp, w_hz)):
-                add(rz1.at[a, 1 : PAIRS + 1, 3 * l + n], w.reshape(PAIRS, 2, NR, WIDTH).at[:, l, rows])
-            for n, w in enumerate((w_er, w_ea, w_eh)):
-                add(rz2.at[a, :, 3 * l + n], w.reshape(PAIRS, 2, NR, WIDTH).at[:, l, rows])
+    for a in range(2):
+        rows = slice(16 * a, 16 * a + 16)
+        for n, w in enumerate((w_hr, w_hp, w_hz)):
+            add(rz1.at[a, 1 : LAYERS + 1, n], w.at[:, rows])
+        for n, w in enumerate((w_er, w_ea, w_eh)):
+            add(rz2.at[a, :, n], w.at[:, rows])
     for d in copies:
         d.start()
     for d in copies:

time: 84.6 us -> 79.9 us (0.944)
  Pallas kernels: 83.8 us -> 79.1 us
    pallas_call x1, Pallas kernels: 79.9 us -> 75.2 us  [local(): step(*(pltpu.with_memory_space_constraint(x, pltpu.HBM) for x in operands))]
where the time goes in v3:
time: 79.9 us; the launch traced here: 79.8 us
  Pallas kernels  79.1 us (99%)
    pallas_call x1, Pallas kernels, local(): step(*(pltpu.with_memory_space_constraint(x, pltpu.HBM) for x in operands))  75.2 us
    pallas_call x1, Pallas kernels, rows_out(): pl.pallas_call(write_kernel, out_shape=tuple((jax.ShapeDtypeStruct((LAYER...  3.95 us

profile of v3, /device:TPU:1, one launch (start us, length us, event | category | flops | bytes accessed | tf_op | source)
XLA Modules:
  0.0 79.8 jit_solution(16829645894809488948)
XLA Ops:
  0.6 75.2 %yee_step.1 = (f32[25,2,104,128]{3,2,1,0:T(8,128)S(1)}, f32[24,96,128]{2,1,0:T(8,128)S(1)}, f32[24,96,128]{2,1,0:T(8,128)S(1)}, f32[24,96,128]{2,1,0:T(8,128)S(1...) custom-call(f32[24,128,128]{2,1,0:T(8,128)} %er_h.1, ...), custom_call_target="tpu_custom_call" | custom-call | tf_op jit(solution)/shard_map/yee_step/pallas_call | solution.py:674
  75.8 3.9 %write_fields.1 = (f32[24,128,128]{2,1,0:T(8,128)}, f32[24,128,128]{2,1,0:T(8,128)}, f32[24,128,128]{2,1,0:T(8,128)}, f32[24,128,128]{2,1,0:T(8,128)}, f32[24,128,128]{2,1,0:T(8,128)}, /*index=5*/f32[24,128,128]{2,1,0:T(8,128)}) custom-call(f32[25,2,104,128]{3,2,1,0:T(8,128)S(1)} %get-tuple-element.13.ho, f32[24,96,128]{2,1,0:T(8,128)S(1)} %get-tuple-element.14.o_hz, ...), custom_call_target="tpu_custom_call" | custom-call | tf_op jit(solution)/shard_map/write_fields/pallas_call | solution.py:680

commit v4 on v3

--- a/solution.py
+++ b/solution.py
@@ -16,7 +16,7 @@
 OUT = NR - NF
 LAYERS = 24
 WIDTH = 128
-CHUNKS = 3
+CHUNKS = 6
 PER_CHUNK = LAYERS // CHUNKS
 HELD = PER_CHUNK // 4
 HALO_R = 32
@@ -29,8 +29,8 @@
 BF16 = jnp.bfloat16
 
 C_DT_RN, C_UP, C_HERE, C_DT_RC, C_RC, C_KEEP_PREV, C_P, C_Q, C_RN = range(9)
-ST_Q, ST_2, ST_C, ST_3, ST_Z = 0, 6, 8, 9, 11
-NSTAGE = 17
+ST_Q, ST_2, ST_C, ST_Z = 0, 6, 8, 9
+NSTAGE = 15
 B_P1O, B_ER, B_EA, B_P2, B_HO, B_P1Q, B_HI = 0, 1, 2, 3, 4, 5, 10
 NBORDER = 20
 
@@ -70,7 +70,7 @@
     perm, cond, cut, base, phase,
     coef, ktab, wts, tab,
     p1s, p1r, p1q, p2s, p2r,
-    g, rq, s, r2, u, ru, t, v1, v2, ki,
+    g, rq, s, r2, u, ru, v1, v2, ki,
     in_sem, send, recv, bsend, brecv,
 ):
     phi = lax.axis_index("phi")
@@ -92,7 +92,6 @@
     up = (gz + 1) % 8
     down = (gz + 7) % 8
     first_bit = (gray, hi_bit)
-    second_bit = (hi_bit, gray)
     first_dev = ((dev_z1, sib_z1), (dev_z3, sib_z3))
     second_dev = (dev_z3, dev_z1)
     pair = tuple(2 * q + b for b in first_bit)
@@ -222,24 +221,14 @@
                 out.append(move(f, c, ST_Q + 3 * a + n, src, rq.at[f, c, a, slots[n]], devs[n]))
         return out
 
-    def eight(bit):
-        return pl.ds(pl.multiple_of(8 * bit, 8), 8)
-
     def d_2(f, c, sets=(0, 1)):
         return [
-            move(f, c, ST_2 + a, s.at[f, c, a, :, :, eight(1 - second_bit[a])], r2.at[f, c, a], second_dev[a])
+            move(f, c, ST_2 + a, s.at[f, c, a], r2.at[f, c, a], second_dev[a])
             for a in sets
         ]
 
     def d_c(f, c):
         return [move(f, c, ST_C, u.at[f, c], ru.at[f, c], dev_y)]
-
-    def d_3(f, c):
-        out = []
-        for a in range(2):
-            own = t.at[f, c, a, :, :, eight(second_bit[a])]
-            out.append(move(f, c, ST_3 + a, own, own, second_dev[a]))
-        return out
 
     def d_z(f, c, sets=(0, 1)):
         out = []
@@ -301,20 +290,14 @@
     def stage_2(f, c):
         arrived(d_2(f, c))
         for a in range(2):
-            u[f, c, a] = s[f, c, a, :, :, eight(second_bit[a])] + r2[f, c, a]
+            u[f, c, a] = s[f, c, a] + r2[f, c, a]
         go(d_c(f, c))
 
-    def stage_3(f, c):
+    def stage_4(f, c):
         arrived(d_c(f, c))
         for a in range(2):
-            w = wts[pl.ds(pl.multiple_of(16 * a + 8 * second_bit[a], 8), 8)]
-            t[f, c, a, :, :, eight(second_bit[a])] = (u[f, c, a] + ru[f, c, a]) * w[None, None]
-        go(d_3(f, c))
-
-    def stage_4(f, c):
-        arrived(d_3(f, c))
-        for a in range(2):
-            x = t[f, c, a].reshape(48 * HELD, 256)
+            w = wts[16 * a : 16 * a + 16]
+            x = ((u[f, c, a] + ru[f, c, a]) * w[None, None]).reshape(48 * HELD, 256)
             k = PER_CHUNK * c + HELD * pair[a]
             if f == 0:
                 y = dot3(x, tab[0, a], tab[1, a], ((1,), (1,))).reshape(HELD, 3, 16, 640)
@@ -521,71 +504,95 @@
     arrived(b_p1q)
 
     order = [
-        (begin_h, 2),
         (outer_loaded,),
         (run, inner_factors, 0, 6),
         (run, inner_factors, 6, 12),
         (run, inner_factors, 12, 18),
+        (begin_h, 2),
+        (stage_1, 0, 0),
+        (begin_h, 3),
+        (stage_1, 0, 1),
         (run, inner_factors, 18, 24),
         (arrived, [b_p1o]),
-        (stage_1, 0, 0),
         (run, outer_h, 21, 24),
         (go, [b_ho]),
         (run, outer_h, 18, 21),
-        (stage_1, 0, 1),
         (run, outer_h, 15, 18),
         (run, outer_h, 12, 15),
+        (begin_h, 4),
         (stage_1, 0, 2),
         (stage_2, 0, 0),
         (run, outer_h, 9, 12),
+        (begin_h, 5),
+        (stage_1, 0, 3),
+        (stage_2, 0, 1),
         (run, outer_h, 6, 9),
         (run, outer_h, 3, 6),
-        (stage_2, 0, 1),
+        (stage_1, 0, 4),
+        (stage_2, 0, 2),
         (run, outer_h, 0, 3),
         (go, [b_p2]),
-        (stage_2, 0, 2),
-        (stage_3, 0, 0),
-        (stage_3, 0, 1),
-        (stage_3, 0, 2),
         (stage_4, 0, 0),
+        (stage_1, 0, 5),
+        (stage_2, 0, 3),
         (stage_4, 0, 1),
+        (stage_2, 0, 4),
         (stage_4, 0, 2),
+        (stage_2, 0, 5),
+        (stage_4, 0, 3),
         (stage_5, 0, 1),
         (stage_5, 0, 0),
         (begin_e, 1),
+        (stage_4, 0, 4),
         (stage_5, 0, 2),
+        (begin_e, 2),
+        (stage_4, 0, 5),
+        (stage_5, 0, 3),
+        (begin_e, 3),
+        (stage_1, 1, 1),
+        (stage_5, 0, 4),
+        (begin_e, 4),
+        (stage_1, 1, 2),
+        (stage_5, 0, 5),
         (layer_below,),
         (begin_e, 0),
-        (begin_e, 2),
+        (begin_e, 5),
         (run, last_inner_row, 0, LAYERS),
+        (stage_1, 1, 3),
+        (stage_2, 1, 1),
         (outer_borders,),
         (run, outer_e, 0, 2),
         (run, outer_e, 2, 4),
+        (stage_1, 1, 4),
+        (stage_2, 1, 2),
         (run, outer_e, 4, 6),
-        (stage_1, 1, 1),
         (run, outer_e, 6, 8),
+        (stage_1, 1, 0),
         (run, outer_e, 8, 10),
-        (stage_1, 1, 0),
+        (stage_1, 1, 5),
+        (stage_4, 1, 1),
+        (stage_2, 1, 3),
+        (stage_2, 1, 4),
         (run, outer_e, 10, 12),
+        (stage_4, 1, 2),
+        (stage_2, 1, 0),
         (run, outer_e, 12, 14),
-        (stage_1, 1, 2),
-        (stage_2, 1, 1),
         (run, outer_e, 14, 16),
+        (stage_2, 1, 5),
         (run, outer_e, 16, 18),
-        (stage_2, 1, 0),
         (run, outer_e, 18, 20),
         (run, outer_e, 20, 22),
+        (stage_4, 1, 3),
         (run, outer_e, 22, 24),
-        (stage_2, 1, 2),
-        (stage_3, 1, 1),
-        (stage_3, 1, 0),
-        (stage_3, 1, 2),
-        (stage_4, 1, 1),
+        (stage_4, 1, 4),
         (stage_4, 1, 0),
-        (stage_4, 1, 2),
+        (stage_4, 1, 5),
         (drain,),
         (stage_5, 1, 1),
         (stage_5, 1, 2),
+        (stage_5, 1, 3),
+        (stage_5, 1, 4),
+        (stage_5, 1, 5),
         (stage_5, 1, 0),
     ]
     for step, *what in order:
@@ -649,9 +656,8 @@
             scratch(2, 2, LAYERS, 3, 16, 128),
             scratch(2, CHUNKS, 2, 3, HELD, 3, 16, 128),
             scratch(2, CHUNKS, 2, HELD, 3, 16, 256),
-            scratch(2, CHUNKS, 2, HELD, 3, 8, 256),
-            scratch(2, CHUNKS, 2, HELD, 3, 8, 256),
-            scratch(2, CHUNKS, 2, HELD, 3, 8, 256),
+            scratch(2, CHUNKS, 2, HELD, 3, 16, 256),
+            scratch(2, CHUNKS, 2, HELD, 3, 16, 256),
             scratch(2, CHUNKS, 2, HELD, 3, 16, 256),
             scratch(CHUNKS, 2, 3, HELD, 4, 16, 128),
             scratch(CHUNKS, 2, 3, HELD, 3, 16, 128),

time: 79.9 us -> 76 us (0.951)
  Pallas kernels: 79.1 us -> 75.3 us
    pallas_call x1, Pallas kernels: 75.2 us -> 71.3 us  [local(): step(*(pltpu.with_memory_space_constraint(x, pltpu.HBM) for x in operands))]
where the time goes in v4:
time: 76 us; the launch traced here: 75.9 us
  Pallas kernels  75.3 us (99%)
    pallas_call x1, Pallas kernels, local(): step(*(pltpu.with_memory_space_constraint(x, pltpu.HBM) for x in operands))  71.3 us
    pallas_call x1, Pallas kernels, rows_out(): pl.pallas_call(write_kernel, out_shape=tuple((jax.ShapeDtypeStruct((LAYER...  3.95 us

profile of v4, /device:TPU:1, one launch (start us, length us, event | category | flops | bytes accessed | tf_op | source)
XLA Modules:
  0.0 75.9 jit_solution(16416054011815221970)
XLA Ops:
  0.6 71.3 %yee_step.1 = (f32[25,2,104,128]{3,2,1,0:T(8,128)S(1)}, f32[24,96,128]{2,1,0:T(8,128)S(1)}, f32[24,96,128]{2,1,0:T(8,128)S(1)}, f32[24,96,128]{2,1,0:T(8,128)S(1...) custom-call(f32[24,128,128]{2,1,0:T(8,128)} %er_h.1, ...), custom_call_target="tpu_custom_call" | custom-call | tf_op jit(solution)/shard_map/yee_step/pallas_call | solution.py:680
  72.0 3.9 %write_fields.1 = (f32[24,128,128]{2,1,0:T(8,128)}, f32[24,128,128]{2,1,0:T(8,128)}, f32[24,128,128]{2,1,0:T(8,128)}, f32[24,128,128]{2,1,0:T(8,128)}, f32[24,128,128]{2,1,0:T(8,128)}, /*index=5*/f32[24,128,128]{2,1,0:T(8,128)}) custom-call(f32[25,2,104,128]{3,2,1,0:T(8,128)S(1)} %get-tuple-element.13.ho, f32[24,96,128]{2,1,0:T(8,128)S(1)} %get-tuple-element.14.o_hz, ...), custom_call_target="tpu_custom_call" | custom-call | tf_op jit(solution)/shard_map/write_fields/pallas_call | solution.py:686

commit v5 on v4

--- a/solution.py
+++ b/solution.py
@@ -506,37 +506,37 @@
     order = [
         (outer_loaded,),
         (run, inner_factors, 0, 6),
-        (run, inner_factors, 6, 12),
-        (run, inner_factors, 12, 18),
         (begin_h, 2),
         (stage_1, 0, 0),
         (begin_h, 3),
         (stage_1, 0, 1),
+        (run, inner_factors, 6, 12),
+        (run, inner_factors, 12, 18),
         (run, inner_factors, 18, 24),
         (arrived, [b_p1o]),
         (run, outer_h, 21, 24),
         (go, [b_ho]),
         (run, outer_h, 18, 21),
-        (run, outer_h, 15, 18),
-        (run, outer_h, 12, 15),
         (begin_h, 4),
         (stage_1, 0, 2),
         (stage_2, 0, 0),
-        (run, outer_h, 9, 12),
+        (run, outer_h, 15, 18),
+        (run, outer_h, 12, 15),
         (begin_h, 5),
         (stage_1, 0, 3),
         (stage_2, 0, 1),
+        (run, outer_h, 9, 12),
+        (stage_1, 0, 4),
         (run, outer_h, 6, 9),
-        (run, outer_h, 3, 6),
-        (stage_1, 0, 4),
         (stage_2, 0, 2),
-        (run, outer_h, 0, 3),
-        (go, [b_p2]),
         (stage_4, 0, 0),
         (stage_1, 0, 5),
+        (run, outer_h, 3, 6),
         (stage_2, 0, 3),
         (stage_4, 0, 1),
         (stage_2, 0, 4),
+        (run, outer_h, 0, 3),
+        (go, [b_p2]),
         (stage_4, 0, 2),
         (stage_2, 0, 5),
         (stage_4, 0, 3),
@@ -559,8 +559,8 @@
         (begin_e, 5),
         (run, last_inner_row, 0, LAYERS),
         (stage_1, 1, 3),
+        (outer_borders,),
         (stage_2, 1, 1),
-        (outer_borders,),
         (run, outer_e, 0, 2),
         (run, outer_e, 2, 4),
         (stage_1, 1, 4),
@@ -568,24 +568,24 @@
         (run, outer_e, 4, 6),
         (run, outer_e, 6, 8),
         (stage_1, 1, 0),
-        (run, outer_e, 8, 10),
         (stage_1, 1, 5),
         (stage_4, 1, 1),
         (stage_2, 1, 3),
+        (run, outer_e, 8, 10),
         (stage_2, 1, 4),
-        (run, outer_e, 10, 12),
         (stage_4, 1, 2),
         (stage_2, 1, 0),
+        (run, outer_e, 10, 12),
         (run, outer_e, 12, 14),
+        (stage_2, 1, 5),
         (run, outer_e, 14, 16),
-        (stage_2, 1, 5),
         (run, outer_e, 16, 18),
+        (stage_4, 1, 3),
         (run, outer_e, 18, 20),
+        (stage_4, 1, 4),
         (run, outer_e, 20, 22),
-        (stage_4, 1, 3),
+        (stage_4, 1, 0),
         (run, outer_e, 22, 24),
-        (stage_4, 1, 4),
-        (stage_4, 1, 0),
         (stage_4, 1, 5),
         (drain,),
         (stage_5, 1, 1),

time: 76 us -> 76.7 us (level)
  no operation moved by 1% of the time
where the time goes in v5:
time: 76.7 us; the launch traced here: 76.6 us
  Pallas kernels  75.9 us (99%)
    pallas_call x1, Pallas kernels, local(): step(*(pltpu.with_memory_space_constraint(x, pltpu.HBM) for x in operands))  72 us
    pallas_call x1, Pallas kernels, rows_out(): pl.pallas_call(write_kernel, out_shape=tuple((jax.ShapeDtypeStruct((LAYER...  3.95 us

profile of v5, /device:TPU:1, one launch (start us, length us, event | category | flops | bytes accessed | tf_op | source)
XLA Modules:
  0.0 76.6 jit_solution(12557793807187331580)
XLA Ops:
  0.6 72.0 %yee_step.1 = (f32[25,2,104,128]{3,2,1,0:T(8,128)S(1)}, f32[24,96,128]{2,1,0:T(8,128)S(1)}, f32[24,96,128]{2,1,0:T(8,128)S(1)}, f32[24,96,128]{2,1,0:T(8,128)S(1...) custom-call(f32[24,128,128]{2,1,0:T(8,128)} %er_h.1, ...), custom_call_target="tpu_custom_call" | custom-call | tf_op jit(solution)/shard_map/yee_step/pallas_call | solution.py:680
  72.6 3.9 %write_fields.1 = (f32[24,128,128]{2,1,0:T(8,128)}, f32[24,128,128]{2,1,0:T(8,128)}, f32[24,128,128]{2,1,0:T(8,128)}, f32[24,128,128]{2,1,0:T(8,128)}, f32[24,128,128]{2,1,0:T(8,128)}, /*index=5*/f32[24,128,128]{2,1,0:T(8,128)}) custom-call(f32[25,2,104,128]{3,2,1,0:T(8,128)S(1)} %get-tuple-element.13.ho, f32[24,96,128]{2,1,0:T(8,128)S(1)} %get-tuple-element.14.o_hz, ...), custom_call_target="tpu_custom_call" | custom-call | tf_op jit(solution)/shard_map/write_fields/pallas_call | solution.py:686
